TPU v7x, 128 devices: a whole 4x4x4 slice. The times are simulated.
128 devices in a mesh: dp: 2 (over core), expert: 64 (over z, y, x).
Axes of the slice: x: 4, y: 4, z: 4, core: 2. Of those that a mesh axis runs over, the one named last changes fastest.
Arguments:
- patches: bfloat16 [10240, 2048], P('expert', 'dp'), may hold values from -6 to 6
- expert_ids: int32 [10240, 2], P('expert'), may hold values from 0 to 63, all different within a row; in each aligned block of 160 rows (0 to 159, 160 to 319, ...) at most 15 rows name the same one
- gate_probs: float32 [10240, 2], P('expert'), may hold values from 0.1 to 1
- out_grad: bfloat16 [10240, 2048], P('expert', 'dp'), may hold values from -6 to 6
- w_gate: bfloat16 [64, 2048, 1024], P('expert', None, 'dp'), may hold values from -0.125 to 0.125
- w_up: bfloat16 [64, 2048, 1024], P('expert', None, 'dp'), may hold values from -0.125 to 0.125
- w_down: bfloat16 [64, 1024, 2048], P('expert', None, 'dp'), may hold values from -0.1875 to 0.1875
Outputs:
- mixed: bfloat16 [10240, 2048], P('expert', 'dp')
- patch_grad: bfloat16 [10240, 2048], P('expert', 'dp')
- w_gate_grad: bfloat16 [64, 2048, 1024], P('expert', None, 'dp')
- w_up_grad: bfloat16 [64, 2048, 1024], P('expert', None, 'dp')
- w_down_grad: bfloat16 [64, 1024, 2048], P('expert', None, 'dp')
Inputs may be any that keep to these rules, and one draw needn't show every extreme that they name: `expert_ids`: the 2 experts of a row differ. Among the 160 rows of one device no expert is named by more than 15 rows, and on some device an expert is named by exactly 15; on every device every expert is named by at least one row.
All inputs are finite; a program needn't handle non-finite values.
Results may differ from a plain program's by a relative error of at most 0.0065.
Values may be sent and summed in bfloat16 or wider, within the bound.
No kernel may reach another device: no remote copies, remote signals or barrier semaphores. Data moves between devices by JAX's collectives and lax.ppermute only.
A program may use at most 128 MiB of HBM per device.

v0:
```python
import jax
import jax.numpy as jnp
from jax import lax
from jax.sharding import PartitionSpec as P

F32 = jnp.float32
BF16 = jnp.bfloat16


def dot(left, right, left_dims, right_dims):
    return lax.dot_general(
        left, right, ((left_dims, right_dims), ((), ())), preferred_element_type=F32
    )


def body(patches, expert_ids, gate_probs, out_grad, w_gate, w_up, w_down):
    tok_rows, width_dev = patches.shape
    top_count = expert_ids.shape[1]
    experts = lax.axis_size("expert")
    cores = lax.axis_size("dp")
    core = lax.axis_index("dp")
    hidden_dev = w_gate.shape[2]
    width = w_gate.shape[1]
    per_core = 8
    core_slots = experts * per_core
    slot_count = cores * core_slots

    def swap(value):
        return lax.ppermute(value, "dp", [(0, 1), (1, 0)])

    def exchange(value):
        return lax.all_to_all(
            value.reshape(cores * experts, per_core, width_dev),
            ("dp", "expert"),
            split_axis=0,
            concat_axis=0,
            tiled=True,
        ).reshape(cores, core_slots, width_dev)

    def in_order(mine, other, axis):
        first = jnp.where(core == 0, mine, other)
        second = jnp.where(core == 0, other, mine)
        return first, second

    flat_ids = expert_ids.reshape(-1)
    onehot = (flat_ids[:, None] == jnp.arange(experts, dtype=jnp.int32)[None, :]).astype(F32)
    route_count = tok_rows * top_count
    before = (
        jnp.arange(route_count, dtype=jnp.int32)[:, None]
        > jnp.arange(route_count, dtype=jnp.int32)[None, :]
    ).astype(BF16)
    earlier = dot(before, onehot.astype(BF16), (1,), (0,))
    ranks = jnp.sum(earlier * onehot, axis=1).astype(jnp.int32)
    slots = ((ranks % 2) * core_slots + flat_ids * per_core + ranks // 2).reshape(
        tok_rows, top_count
    )
    positions = jnp.arange(slot_count, dtype=jnp.int32)[:, None]
    hits = [positions == slots[None, :, k] for k in range(top_count)]
    select = (hits[0] | hits[1]).astype(BF16)
    slot_probs = sum(
        jnp.sum(jnp.where(hits[k], gate_probs[None, :, k], 0.0), axis=1, keepdims=True)
        for k in range(top_count)
    )

    sent_rows = dot(select, patches, (1,), (0,)).astype(BF16)
    rows = exchange(sent_rows)
    sent_grads = (dot(select, out_grad, (1,), (0,)) * slot_probs).astype(BF16)
    grads = exchange(sent_grads)

    gate_lo, gate_hi = in_order(w_gate[0], swap(w_gate[0]), 1)
    up_lo, up_hi = in_order(w_up[0], swap(w_up[0]), 1)
    pair_weights = jnp.concatenate([gate_lo, gate_hi, up_lo, up_hi], axis=1)
    down_weights = jnp.stack(in_order(w_down[0], swap(w_down[0]), 1), axis=0)
    hidden_all = cores * hidden_dev

    rows_full = jnp.concatenate([rows[0], rows[1]], axis=1)
    projected = dot(rows_full, pair_weights, (1,), (0,))
    gate_pre = projected[:, :hidden_all]
    up_pre = projected[:, hidden_all:]
    sigma = jax.nn.sigmoid(gate_pre)
    hidden = (gate_pre * sigma * up_pre).astype(BF16)
    expert_out = jnp.stack(
        [dot(hidden, down_weights[i], (1,), (0,)).astype(BF16) for i in range(cores)], axis=0
    )
    back_out = exchange(expert_out).reshape(slot_count, width_dev)

    hidden_grad = sum(dot(grads[i], down_weights[i], (1,), (1,)) for i in range(cores))
    gate_grad = (hidden_grad * up_pre * sigma * (1.0 + gate_pre * (1.0 - sigma))).astype(BF16)
    up_grad = (hidden_grad * gate_pre * sigma).astype(BF16)
    pair_grad = jnp.concatenate([gate_grad, up_grad], axis=1)
    dx_slots = jnp.stack(
        [
            dot(
                pair_grad, pair_weights[i * width_dev : (i + 1) * width_dev], (1,), (1,)
            ).astype(BF16)
            for i in range(cores)
        ],
        axis=0,
    )
    back_grad = exchange(dx_slots).reshape(slot_count, width_dev)

    rows_other = swap(rows_full)
    hidden_other = swap(hidden)
    grads_mine, grads_send = in_order(grads[0], grads[1], 1)
    grads_other = swap(grads_send)
    down_grad = (
        dot(hidden, grads_mine, (0,), (0,)) + dot(hidden_other, grads_other, (0,), (0,))
    ).astype(BF16)

    def share(value):
        return in_order(value[:, :hidden_dev], value[:, hidden_dev:], 1)

    gate_mine, gate_send = share(gate_grad)
    up_mine, up_send = share(up_grad)
    gate_other = swap(gate_send)
    up_other = swap(up_send)

    def row_grad(mine, other):
        return (
            dot(rows_full, mine, (0,), (0,)) + dot(rows_other, other, (0,), (0,))
        ).astype(BF16)

    gate_wgrad = row_grad(gate_mine, gate_other)
    up_wgrad = row_grad(up_mine, up_other)

    picked = [
        dot(hits[k].astype(BF16), back_out, (0,), (0,)) * gate_probs[:, k : k + 1]
        for k in range(top_count)
    ]
    mixed = (picked[0] + picked[1]).astype(BF16)
    patch_grad = dot(select, back_grad, (0,), (0,)).astype(BF16)
    return mixed, patch_grad, gate_wgrad[None], up_wgrad[None], down_grad[None]


def solution(mesh):
    in_specs = (
        P("expert", "dp"),
        P("expert", None),
        P("expert", None),
        P("expert", "dp"),
        P("expert", None, "dp"),
        P("expert", None, "dp"),
        P("expert", None, "dp"),
    )
    out_specs = (
        P("expert", "dp"),
        P("expert", "dp"),
        P("expert", None, "dp"),
        P("expert", None, "dp"),
        P("expert", None, "dp"),
    )
    return jax.shard_map(body, mesh=mesh, in_specs=in_specs, out_specs=out_specs, check_vma=False)
```

profile of v0, /device:TPU:1, one launch (start us, length us, event | category | flops | bytes accessed | tf_op | source)
XLA Modules:
  0.0 180.2 jit_solution(8571288559314179074)
XLA Ops:
  2.8 2.2 %convert_bitcast_fusion = bf16[128,8,1024]{2,1,0:T(8,128)(2,1)} fusion(bf16[160,1024]{1,0:T(8,128)(2,1)S(1)} %copy-done, s32[160]{0:T(256)S(1)} %bitcast.112, s32[160]{0:T(256)S(1)} %bitcast.107), kind=kOutput, calls=%fused_computation.25 | convolution fusion | flops 337084416 | bytes 2426112 | tf_op jit(solution)/shard_map/dot_general | solution.py:11
  5.1 11.5 %all-to-all-start = ((bf16[128,8,1024]{2,1,0:T(8,128)(2,1)}), bf16[128,8,1024]{2,1,0:T(8,128)(2,1)S(1)}, u32[]{:S(2)}, u32[]{:S(2)}) async-start(bf16[128,8,1024]{2,1,0:T(8,128)(2,1)} %convert_bitcast_fusion), calls=%async_computation | async-start | bytes 4194304 | tf_op jit(solution)/shard_map/all_to_all | solution.py:32
  18.5 2.2 %fusion.13 = bf16[128,8,1024]{2,1,0:T(8,128)(2,1)} fusion(f32[1024]{0:T(1024)S(1)} %add.51, bf16[160,1024]{1,0:T(8,128)(2,1)S(1)} %copy-done.17, s32[160]{0:T(256)S(1)} %bitcast.114, s32[160]{0:T(256)S(1)} %bitcast.109), kind=kOutput, calls=%fused_computation.33 | convolution fusion | flops 338132992 | bytes 2430208 | tf_op jit(solution)/shard_map/dot_general | solution.py:11
  20.7 24.5 %all-to-all-done = bf16[128,8,1024]{2,1,0:T(8,128)(2,1)S(1)} async-done(((bf16[128,8,1024]{2,1,0:T(8,128)(2,1)}), bf16[128,8,1024]{2,1,0:T(8,128)(2,1)S(1)}, u32[]{:S(2)}, u32[]{:S(2)}) %all-to-all-start) | async-done | bytes 2097184 | tf_op jit(solution)/shard_map/all_to_all | solution.py:32
  46.5 6.0 %all-to-all-start.2 = ((bf16[128,8,1024]{2,1,0:T(8,128)(2,1)}), bf16[128,8,1024]{2,1,0:T(8,128)(2,1)S(1)}, u32[]{:S(2)}, u32[]{:S(2)}) async-start(bf16[128,8,1024]{2,1,0:T(8,128)(2,1)} %fusion.13), calls=%async_computation.2 | async-start | bytes 4194304 | tf_op jit(solution)/shard_map/all_to_all | solution.py:32
  52.6 1.9 %slice_bitcast_fusion.3 = (bf16[512,1024]{1,0:T(8,128)(2,1)S(1)}, bf16[512,1024]{1,0:T(8,128)(2,1)S(1)}) fusion(bf16[128,8,1024]{2,1,0:T(8,128)(2,1)} %copy-done.6), kind=kLoop, calls=%fused_computation.53 | loop fusion | bytes 4194304 | tf_op jit(solution)/shard_map/squeeze | solution.py:76
  54.8 2.7 %broadcast_select_fusion.3 = (bf16[2048,512]{1,0:T(8,128)(2,1)S(1)}, bf16[2048,512]{1,0:T(8,128)(2,1)S(1)}) fusion(bf16[2048,512]{1,0:T(8,128)(2,1)} %collective-permute-done.1, pred[]{:T(512)S(6)} %eq.73, bf16[1,2048,512]{2,1,0:T(8,128)(2,1)S(1)} %copy-done.10), kind=kLoop, calls=%fused_computation.29 | loop fusion | flops 2097152 | bytes 8388609 | tf_op jit(solution)/shard_map/jit(_where)/select_n | solution.py:41
  57.5 2.1 %broadcast_select_fusion.5 = (bf16[2048,512]{1,0:T(8,128)(2,1)S(1)}, bf16[2048,512]{1,0:T(8,128)(2,1)S(1)}) fusion(bf16[2048,512]{1,0:T(8,128)(2,1)} %collective-permute-done, pred[]{:T(512)S(6)} %eq.73, bf16[1,2048,512]{2,1,0:T(8,128)(2,1)S(1)} %copy-done.11), kind=kLoop, calls=%fused_computation.31 | loop fusion | flops 2097152 | bytes 8388609 | tf_op jit(solution)/shard_map/jit(_where)/select_n | solution.py:41
  60.9 3.3 %copy-done.2 = bf16[2048,2048]{1,0:T(8,128)(2,1)} copy-done((bf16[2048,2048]{1,0:T(8,128)(2,1)}, bf16[2048,2048]{1,0:T(8,128)(2,1)S(1)}, u32[]{:S(2)}) %copy-start.2) | copy-done | bytes 8388632
  64.1 6.2 %fusion.80 = f32[512,2048]{1,0:T(8,128)} fusion(bf16[2048,2048]{1,0:T(8,128)(2,1)S(1)} %pad_maximum_fusion, bf16[512,1024]{1,0:T(8,128)(2,1)S(1)} %get-tuple-element.13, bf16[512,1024]{1,0:T(8,128)(2,1)S(1)} %get-tuple-element.12), kind=kOutput, calls=%fused_computation.102 | convolution fusion | flops 4299161600 | bytes 14680064 | tf_op jit(solution)/shard_map/dot_general | solution.py:11
  70.4 10.9 %all-to-all-done.2 = bf16[128,8,1024]{2,1,0:T(8,128)(2,1)S(1)} async-done(((bf16[128,8,1024]{2,1,0:T(8,128)(2,1)}), bf16[128,8,1024]{2,1,0:T(8,128)(2,1)S(1)}, u32[]{:S(2)}, u32[]{:S(2)}) %all-to-all-start.2) | async-done | bytes 2097184 | tf_op jit(solution)/shard_map/all_to_all | solution.py:32
  81.2 3.7 %fusion.47 = f32[512,1024]{1,0:T(8,128)S(1)} fusion(bf16[128,8,1024]{2,1,0:T(8,128)(2,1)S(1)} %all-to-all-done.2, bf16[1024,1024]{1,0:T(8,128)(2,1)} %collective-permute-done.2, pred[]{:T(512)S(6)} %eq.73, bf16[1,1024,1024]{2,1,0:T(8,128)(2,1)} %param.13), kind=kOutput, calls=%fused_computation.58 | convolution fusion | flops 1074790400 | bytes 7340033 | tf_op jit(solution)/shard_map/dot_general | solution.py:11
  85.4 5.5 %multiply_convert_fusion.2 = (bf16[512,1024]{1,0:T(8,128)(2,1)}, bf16[512,1024]{1,0:T(8,128)(2,1)}, bf16[512,1024]{1,0:T(8,128)(2,1)}) fusion(f32[512,2048]{1,0:T(8,128)S(1)} %copy-done.19, f32[512,1024]{1,0:T(8,128)S(1)} %fusion.47, bf16[1024,1024]{1,0:T(8,128)(2,1)} %collective-permute-done.2, pred[]{:T(512)S(6)} %eq.73, ...), kind=kOutput, calls=%fused_computation.22 | convolution fusion | flops 1083703296 | bytes 14680065 | tf_op jit(solution)/shard_map/dot_general | solution.py:11
  90.9 2.5 %fusion.27 = bf16[1,512,1024]{2,1,0:T(8,128)(2,1)S(1)} fusion(bf16[512,1024]{1,0:T(8,128)(2,1)} %get-tuple-element.7, bf16[1024,1024]{1,0:T(8,128)(2,1)} %collective-permute-done.2, pred[]{:T(512)S(6)} %eq.73, bf16[1,1024,1024]{2,1,0:T(8,128)(2,1)S(1)} %copy-done.16), kind=kOutput, calls=%fused_computation.42 | convolution fusion | flops 1075314688 | bytes 6291457 | tf_op jit(solution)/shard_map/dot_general | solution.py:11
  93.5 3.2 %fusion.26 = bf16[1,512,1024]{2,1,0:T(8,128)(2,1)S(1)} fusion(bf16[512,1024]{1,0:T(8,128)(2,1)} %get-tuple-element.7, bf16[1024,1024]{1,0:T(8,128)(2,1)} %collective-permute-done.2, pred[]{:T(512)S(6)} %eq.73, bf16[1,1024,1024]{2,1,0:T(8,128)(2,1)S(1)} %copy-done.16), kind=kOutput, calls=%fused_computation.41 | convolution fusion | flops 1075314688 | bytes 6291457 | tf_op jit(solution)/shard_map/dot_general | solution.py:11
  96.7 1.5 pad_maximum_fusion.2
  98.2 5.4 %all-to-all-start.1 = ((bf16[128,8,1024]{2,1,0:T(8,128)(2,1)}), bf16[128,8,1024]{2,1,0:T(8,128)(2,1)S(1)}, u32[]{:S(2)}, u32[]{:S(2)}) async-start(bf16[128,8,1024]{2,1,0:T(8,128)(2,1)} %bitcast.104), calls=%async_computation.1 | async-start | bytes 4194304 | tf_op jit(solution)/shard_map/all_to_all | solution.py:32
  103.6 2.9 %pad_maximum_fusion.1 = bf16[512,2048]{1,0:T(8,128)(2,1)} fusion(bf16[512,1024]{1,0:T(8,128)(2,1)} %copy-done.7, bf16[512,1024]{1,0:T(8,128)(2,1)S(1)} %get-tuple-element.12), kind=kLoop, calls=%fused_computation.11 | loop fusion | flops 4194304 | bytes 4194304 | tf_op jit(solution)/shard_map/concatenate | solution.py:76
  109.2 4.7 %fusion.20 = bf16[1,512,1024]{2,1,0:T(8,128)(2,1)S(1)} fusion(bf16[2048,2048]{1,0:T(8,128)(2,1)} %copy-done.2, bf16[512,1024]{1,0:T(8,128)(2,1)S(1)} %copy-done.12, bf16[512,1024]{1,0:T(8,128)(2,1)S(1)} %copy-done.14), kind=kOutput, calls=%fused_computation.39 | convolution fusion | flops 2152202240 | bytes 7340032 | tf_op jit(solution)/shard_map/dot_general | solution.py:11
  114.0 2.4 %fusion.23 = bf16[1,512,1024]{2,1,0:T(8,128)(2,1)S(1)} fusion(bf16[2048,2048]{1,0:T(8,128)(2,1)S(1)} %bitcast.102, bf16[512,1024]{1,0:T(8,128)(2,1)S(1)} %copy-done.12, bf16[512,1024]{1,0:T(8,128)(2,1)S(1)} %copy-done.14), kind=kOutput, calls=%fused_computation.40 | convolution fusion | flops 2152202240 | bytes 7340032 | tf_op jit(solution)/shard_map/dot_general | solution.py:11
  117.9 3.3 %fusion.51 = f32[2048,512]{1,0:T(8,128)} fusion(pred[]{:T(512)S(6)} %eq.73, bf16[512,1024]{1,0:T(8,128)(2,1)S(1)} %copy-done.14, bf16[512,1024]{1,0:T(8,128)(2,1)S(1)} %copy-done.8, bf16[512,1024]{1,0:T(8,128)(2,1)S(1)} %get-tuple-element.12), kind=kOutput, calls=%fused_computation.66 | convolution fusion | flops 1078198272 | bytes 7340033 | tf_op jit(solution)/shard_map/dot_general | solution.py:11
  121.2 11.1 %all-to-all-done.1 = bf16[128,8,1024]{2,1,0:T(8,128)(2,1)S(1)} async-done(((bf16[128,8,1024]{2,1,0:T(8,128)(2,1)}), bf16[128,8,1024]{2,1,0:T(8,128)(2,1)S(1)}, u32[]{:S(2)}, u32[]{:S(2)}) %all-to-all-start.1) | async-done | bytes 2097184 | tf_op jit(solution)/shard_map/all_to_all | solution.py:32
  132.3 6.5 %all-to-all-start.3 = ((bf16[128,8,1024]{2,1,0:T(8,128)(2,1)}), bf16[128,8,1024]{2,1,0:T(8,128)(2,1)}, u32[]{:S(2)}, u32[]{:S(2)}) async-start(bf16[128,8,1024]{2,1,0:T(8,128)(2,1)} %bitcast.103), calls=%async_computation.3 | async-start | bytes 4194304 | tf_op jit(solution)/shard_map/all_to_all | solution.py:32
  138.8 2.2 %broadcast_select_fusion.12 = bf16[512,512]{1,0:T(8,128)(2,1)} fusion(pred[]{:T(512)S(6)} %eq.73, bf16[512,1024]{1,0:T(8,128)(2,1)} %get-tuple-element.5), kind=kLoop, calls=%fused_computation.70 | loop fusion | flops 262144 | bytes 1572865 | tf_op jit(solution)/shard_map/jit(_where)/select_n | solution.py:42
  141.0 2.1 %broadcast_select_fusion.11 = bf16[512,512]{1,0:T(8,128)(2,1)} fusion(pred[]{:T(512)S(6)} %eq.73, bf16[512,1024]{1,0:T(8,128)(2,1)} %get-tuple-element.6), kind=kLoop, calls=%fused_computation.68 | loop fusion | flops 262144 | bytes 1572865 | tf_op jit(solution)/shard_map/jit(_where)/select_n | solution.py:42
  144.2 3.4 %fusion.49 = f32[2048,512]{1,0:T(8,128)} fusion(pred[]{:T(512)S(6)} %eq.73, bf16[512,1024]{1,0:T(8,128)(2,1)S(1)} %copy-done.13, bf16[512,1024]{1,0:T(8,128)(2,1)S(1)} %copy-done.9, bf16[512,1024]{1,0:T(8,128)(2,1)S(1)} %get-tuple-element.12), kind=kOutput, calls=%fused_computation.64 | convolution fusion | flops 1078198272 | bytes 7340033 | tf_op jit(solution)/shard_map/dot_general | solution.py:11
  147.6 2.5 %fusion.44 = f32[1024,1024]{1,0:T(8,128)S(1)} fusion(bf16[512,1024]{1,0:T(8,128)(2,1)} %get-tuple-element.7, pred[]{:T(512)S(6)} %eq.73, bf16[128,8,1024]{2,1,0:T(8,128)(2,1)S(1)} %copy-done.5), kind=kOutput, calls=%fused_computation.54 | convolution fusion | flops 1074266112 | bytes 7340033 | tf_op jit(solution)/shard_map/dot_general | solution.py:11
  150.1 4.2 %fusion.12 = bf16[1,1024,1024]{2,1,0:T(8,128)(2,1)} fusion(f32[1024,1024]{1,0:T(8,128)S(1)} %fusion.44, bf16[512,1024]{1,0:T(8,128)(2,1)} %collective-permute-done.6, bf16[512,1024]{1,0:T(8,128)(2,1)} %collective-permute-done.7), kind=kOutput, calls=%fused_computation.32 | convolution fusion | flops 1075838976 | bytes 8388608 | tf_op jit(solution)/shard_map/dot_general | solution.py:11
  156.2 10.9 %all-to-all-done.3 = bf16[128,8,1024]{2,1,0:T(8,128)(2,1)} async-done(((bf16[128,8,1024]{2,1,0:T(8,128)(2,1)}), bf16[128,8,1024]{2,1,0:T(8,128)(2,1)}, u32[]{:S(2)}, u32[]{:S(2)}) %all-to-all-start.3) | async-done | bytes 2097184 | tf_op jit(solution)/shard_map/all_to_all | solution.py:32
  167.1 2.9 %fusion.40 = bf16[160,1024]{1,0:T(8,128)(2,1)} fusion(bf16[128,8,1024]{2,1,0:T(8,128)(2,1)} %all-to-all-done.3, s32[160]{0:T(256)S(1)} %bitcast.116, s32[160]{0:T(256)S(1)} %bitcast.111), kind=kOutput, calls=%fused_computation.47 | convolution fusion | flops 336199680 | bytes 2426112 | tf_op jit(solution)/shard_map/dot_general | solution.py:11
  170.0 5.7 %fusion.4 = bf16[1,2048,512]{2,1,0:T(8,128)(2,1)} fusion(f32[2048,512]{1,0:T(8,128)} %fusion.51, bf16[512,2048]{1,0:T(8,128)(2,1)} %collective-permute-done.3, bf16[512,512]{1,0:T(8,128)(2,1)} %collective-permute-done.4), kind=kOutput, calls=%fused_computation.9 | convolution fusion | flops 1075838976 | bytes 8912896 | tf_op jit(solution)/shard_map/dot_general | solution.py:11
  175.7 4.4 %fusion.5 = bf16[1,2048,512]{2,1,0:T(8,128)(2,1)} fusion(f32[2048,512]{1,0:T(8,128)S(1)} %copy-done.18, bf16[512,2048]{1,0:T(8,128)(2,1)} %collective-permute-done.3, bf16[512,512]{1,0:T(8,128)(2,1)} %collective-permute-done.5), kind=kOutput, calls=%fused_computation.10 | convolution fusion | flops 1075838976 | bytes 8912896 | tf_op jit(solution)/shard_map/dot_general | solution.py:11
  (76 shorter events, 14.6 us)
Async XLA Ops:
  0.6 2.2 %copy-start = (bf16[160,1024]{1,0:T(8,128)(2,1)S(1)}, bf16[160,1024]{1,0:T(8,128)(2,1)}, u32[]{:S(2)}) copy-start(bf16[160,1024]{1,0:T(8,128)(2,1)} %param.7) | copy-start | bytes 983044
  5.1 13.2 %copy-start.15 = (f32[160,2]{0,1:T(2,128)S(1)}, f32[160,2]{0,1:T(2,128)}, u32[]{:S(2)}) copy-start(f32[160,2]{0,1:T(2,128)} %param.9) | copy-start | bytes 3844
  5.1 13.4 %copy-start.17 = (bf16[160,1024]{1,0:T(8,128)(2,1)S(1)}, bf16[160,1024]{1,0:T(8,128)(2,1)}, u32[]{:S(2)}) copy-start(bf16[160,1024]{1,0:T(8,128)(2,1)} %param.10) | copy-start | bytes 983044
  5.1 40.2 %all-to-all-start = ((bf16[128,8,1024]{2,1,0:T(8,128)(2,1)}), bf16[128,8,1024]{2,1,0:T(8,128)(2,1)S(1)}, u32[]{:S(2)}, u32[]{:S(2)}) async-start(bf16[128,8,1024]{2,1,0:T(8,128)(2,1)} %convert_bitcast_fusion), calls=%async_computation | async-start | bytes 4194304 | tf_op jit(solution)/shard_map/all_to_all | solution.py:32
  16.5 37.9 %collective-permute-start.1 = (bf16[2048,512]{1,0:T(8,128)(2,1)}, bf16[2048,512]{1,0:T(8,128)(2,1)}, u32[]{:S(2)}, u32[]{:S(2)}) collective-permute-start(bf16[2048,512]{1,0:T(8,128)(2,1)} %bitcast.105), channel_id=1, source_target_pairs={{0,64},{64,0},{1,65},{65,1},{2,66},{66,2},{3,67},{67,3},{4,68},{68... | collective-permute-start | bytes 6291464 | tf_op jit(solution)/shard_map/ppermute | solution.py:29
  17.7 39.8 %collective-permute-start = (bf16[2048,512]{1,0:T(8,128)(2,1)}, bf16[2048,512]{1,0:T(8,128)(2,1)}, u32[]{:S(2)}, u32[]{:S(2)}) collective-permute-start(bf16[2048,512]{1,0:T(8,128)(2,1)} %bitcast.106), channel_id=1, source_target_pairs={{0,64},{64,0},{1,65},{65,1},{2,66},{66,2},{3,67},{67,3},{4,68},{68... | collective-permute-start | bytes 6291464 | tf_op jit(solution)/shard_map/ppermute | solution.py:29
  17.8 63.4 %collective-permute-start.2 = (bf16[1024,1024]{1,0:T(8,128)(2,1)}, bf16[1024,1024]{1,0:T(8,128)(2,1)}, u32[]{:S(2)}, u32[]{:S(2)}) collective-permute-start(bf16[1024,1024]{1,0:T(8,128)(2,1)} %bitcast.121), channel_id=1, source_target_pairs={{0,64},{64,0},{1,65},{65,1},{2,66},{66,2},{3,67},{67,3},{4,68},{68... | collective-permute-start | bytes 6291464 | tf_op jit(solution)/shard_map/ppermute | solution.py:29
  46.5 34.7 %all-to-all-start.2 = ((bf16[128,8,1024]{2,1,0:T(8,128)(2,1)}), bf16[128,8,1024]{2,1,0:T(8,128)(2,1)S(1)}, u32[]{:S(2)}, u32[]{:S(2)}) async-start(bf16[128,8,1024]{2,1,0:T(8,128)(2,1)} %fusion.13), calls=%async_computation.2 | async-start | bytes 4194304 | tf_op jit(solution)/shard_map/all_to_all | solution.py:32
  52.6 2.2 %copy-start.10 = (bf16[1,2048,512]{2,1,0:T(8,128)(2,1)S(1)}, bf16[1,2048,512]{2,1,0:T(8,128)(2,1)}, u32[]{:S(2)}) copy-start(bf16[1,2048,512]{2,1,0:T(8,128)(2,1)} %param.12) | copy-start | bytes 6291460
  54.4 6.4 %copy-start.7 = (bf16[512,1024]{1,0:T(8,128)(2,1)}, bf16[512,1024]{1,0:T(8,128)(2,1)S(1)}, u32[]{:S(2)}) copy-start(bf16[512,1024]{1,0:T(8,128)(2,1)S(1)} %get-tuple-element.13) | copy-start | bytes 3145732
  54.4 3.0 %copy-start.11 = (bf16[1,2048,512]{2,1,0:T(8,128)(2,1)S(1)}, bf16[1,2048,512]{2,1,0:T(8,128)(2,1)}, u32[]{:S(2)}) copy-start(bf16[1,2048,512]{2,1,0:T(8,128)(2,1)} %param.11) | copy-start | bytes 6291460
  60.9 3.3 %copy-start.2 = (bf16[2048,2048]{1,0:T(8,128)(2,1)}, bf16[2048,2048]{1,0:T(8,128)(2,1)S(1)}, u32[]{:S(2)}) copy-start(bf16[2048,2048]{1,0:T(8,128)(2,1)S(1)} %pad_maximum_fusion) | copy-start | bytes 25165828
  81.2 3.7 %copy-start.3 = (bf16[128,8,1024]{2,1,0:T(8,128)(2,1)}, bf16[128,8,1024]{2,1,0:T(8,128)(2,1)S(1)}, u32[]{:S(2)}) copy-start(bf16[128,8,1024]{2,1,0:T(8,128)(2,1)S(1)} %all-to-all-done.2) | copy-start | bytes 6291460
  81.2 3.7 %copy-start.16 = (bf16[1,1024,1024]{2,1,0:T(8,128)(2,1)S(1)}, bf16[1,1024,1024]{2,1,0:T(8,128)(2,1)}, u32[]{:S(2)}) copy-start(bf16[1,1024,1024]{2,1,0:T(8,128)(2,1)} %param.13) | copy-start | bytes 6291460
  81.2 4.2 %copy-start.19 = (f32[512,2048]{1,0:T(8,128)S(1)}, f32[512,2048]{1,0:T(8,128)}, u32[]{:S(2)}) copy-start(f32[512,2048]{1,0:T(8,128)} %fusion.80) | copy-start | bytes 12582916
  98.2 34.1 %all-to-all-start.1 = ((bf16[128,8,1024]{2,1,0:T(8,128)(2,1)}), bf16[128,8,1024]{2,1,0:T(8,128)(2,1)S(1)}, u32[]{:S(2)}, u32[]{:S(2)}) async-start(bf16[128,8,1024]{2,1,0:T(8,128)(2,1)} %bitcast.104), calls=%async_computation.1 | async-start | bytes 4194304 | tf_op jit(solution)/shard_map/all_to_all | solution.py:32
  103.6 4.0 %copy-start.4 = (bf16[128,8,1024]{2,1,0:T(8,128)(2,1)S(1)}, bf16[128,8,1024]{2,1,0:T(8,128)(2,1)}, u32[]{:S(2)}) copy-start(bf16[128,8,1024]{2,1,0:T(8,128)(2,1)} %copy-done.3) | copy-start | bytes 6291460
  106.6 2.7 %copy-start.12 = (bf16[512,1024]{1,0:T(8,128)(2,1)S(1)}, bf16[512,1024]{1,0:T(8,128)(2,1)}, u32[]{:S(2)}) copy-start(bf16[512,1024]{1,0:T(8,128)(2,1)} %get-tuple-element.6) | copy-start | bytes 3145732
  106.6 2.7 %copy-start.14 = (bf16[512,1024]{1,0:T(8,128)(2,1)S(1)}, bf16[512,1024]{1,0:T(8,128)(2,1)}, u32[]{:S(2)}) copy-start(bf16[512,1024]{1,0:T(8,128)(2,1)} %get-tuple-element.5) | copy-start | bytes 3145732
  106.6 63.4 %collective-permute-start.3 = (bf16[512,2048]{1,0:T(8,128)(2,1)}, bf16[512,2048]{1,0:T(8,128)(2,1)}, u32[]{:S(2)}, u32[]{:S(2)}) collective-permute-start(bf16[512,2048]{1,0:T(8,128)(2,1)} %pad_maximum_fusion.1), channel_id=1, source_target_pairs={{0,64},{64,0},{1,65},{65,1},{2,66},{66,2},{3,67},{67,3},{4,68},{68... | collective-permute-start | bytes 6291464 | tf_op jit(solution)/shard_map/ppermute | solution.py:29
  107.6 6.3 %slice-start = ((s8[8388608]{0:T(1024)(128)(4,1)}), s8[4194304]{0:T(1024)(128)(4,1)S(1)}, s32[]{:S(2)}) async-start(s8[8388608]{0:T(1024)(128)(4,1)} %bitcast.101), calls=%async_computation.4 | async-start | bytes 8388608
  108.7 41.4 %collective-permute-start.7 = (bf16[512,1024]{1,0:T(8,128)(2,1)}, bf16[512,1024]{1,0:T(8,128)(2,1)}, u32[]{:S(2)}, u32[]{:S(2)}) collective-permute-start(bf16[512,1024]{1,0:T(8,128)(2,1)} %broadcast_select_fusion.6), channel_id=1, source_target_pairs={{0,64},{64,0},{1,65},{65,1},{2,66},{66,2},{3,67},{67,3},{4,68},{68... | collective-permute-start | bytes 3145736 | tf_op jit(solution)/shard_map/ppermute | solution.py:29
  108.7 41.4 %collective-permute-start.6 = (bf16[512,1024]{1,0:T(8,128)(2,1)}, bf16[512,1024]{1,0:T(8,128)(2,1)}, u32[]{:S(2)}, u32[]{:S(2)}) collective-permute-start(bf16[512,1024]{1,0:T(8,128)(2,1)} %get-tuple-element.7), channel_id=1, source_target_pairs={{0,64},{64,0},{1,65},{65,1},{2,66},{66,2},{3,67},{67,3},{4,68},{68... | collective-permute-start | bytes 3145736 | tf_op jit(solution)/shard_map/ppermute | solution.py:29
  109.2 4.7 %slice-start.1 = ((s8[8388608]{0:T(1024)(128)(4,1)}), s8[4194304]{0:T(1024)(128)(4,1)S(1)}, s32[]{:S(2)}) async-start(s8[8388608]{0:T(1024)(128)(4,1)} %bitcast.101), calls=%async_computation.5 | async-start | bytes 8388608
  132.3 34.8 %all-to-all-start.3 = ((bf16[128,8,1024]{2,1,0:T(8,128)(2,1)}), bf16[128,8,1024]{2,1,0:T(8,128)(2,1)}, u32[]{:S(2)}, u32[]{:S(2)}) async-start(bf16[128,8,1024]{2,1,0:T(8,128)(2,1)} %bitcast.103), calls=%async_computation.3 | async-start | bytes 4194304 | tf_op jit(solution)/shard_map/all_to_all | solution.py:32
  138.8 5.4 %copy-start.9 = (bf16[512,1024]{1,0:T(8,128)(2,1)S(1)}, bf16[512,1024]{1,0:T(8,128)(2,1)}, u32[]{:S(2)}) copy-start(bf16[512,1024]{1,0:T(8,128)(2,1)} %copy-done.7) | copy-start | bytes 3145732
  138.8 5.4 %copy-start.13 = (bf16[512,1024]{1,0:T(8,128)(2,1)S(1)}, bf16[512,1024]{1,0:T(8,128)(2,1)}, u32[]{:S(2)}) copy-start(bf16[512,1024]{1,0:T(8,128)(2,1)} %get-tuple-element.6) | copy-start | bytes 3145732
  143.1 4.5 %copy-start.5 = (bf16[128,8,1024]{2,1,0:T(8,128)(2,1)S(1)}, bf16[128,8,1024]{2,1,0:T(8,128)(2,1)}, u32[]{:S(2)}) copy-start(bf16[128,8,1024]{2,1,0:T(8,128)(2,1)} %copy-done.3) | copy-start | bytes 6291460
  143.1 26.9 %collective-permute-start.4 = (bf16[512,512]{1,0:T(8,128)(2,1)}, bf16[512,512]{1,0:T(8,128)(2,1)}, u32[]{:S(2)}, u32[]{:S(2)}) collective-permute-start(bf16[512,512]{1,0:T(8,128)(2,1)} %broadcast_select_fusion.12), channel_id=1, source_target_pairs={{0,64},{64,0},{1,65},{65,1},{2,66},{66,2},{3,67},{67,3},{4,68},{68... | collective-permute-start | bytes 1572872 | tf_op jit(solution)/shard_map/ppermute | solution.py:29
  144.2 31.5 %collective-permute-start.5 = (bf16[512,512]{1,0:T(8,128)(2,1)}, bf16[512,512]{1,0:T(8,128)(2,1)}, u32[]{:S(2)}, u32[]{:S(2)}) collective-permute-start(bf16[512,512]{1,0:T(8,128)(2,1)} %broadcast_select_fusion.11), channel_id=1, source_target_pairs={{0,64},{64,0},{1,65},{65,1},{2,66},{66,2},{3,67},{67,3},{4,68},{68... | collective-permute-start | bytes 1572872 | tf_op jit(solution)/shard_map/ppermute | solution.py:29
  170.0 5.8 %copy-start.18 = (f32[2048,512]{1,0:T(8,128)S(1)}, f32[2048,512]{1,0:T(8,128)}, u32[]{:S(2)}) copy-start(f32[2048,512]{1,0:T(8,128)} %fusion.49) | copy-start | bytes 12582916
  175.7 4.4 %copy-start.1 = (bf16[160,1024]{1,0:T(8,128)(2,1)S(1)}, bf16[160,1024]{1,0:T(8,128)(2,1)}, u32[]{:S(2)}) copy-start(bf16[160,1024]{1,0:T(8,128)(2,1)} %param.7) | copy-start | bytes 983044
  (2 other events, 2.8 us)
where the time goes:
time: 181 us; the launch traced here: 180 us
  matrix products  61.3 us (34%)
  waiting for transfers between devices  57.4 us (32%)
  starting transfers between devices  33.8 us (19%)
  other arithmetic  18.3 us (10%)
  local copies, waits for them, and re-layouts  8.5 us (5%)
    dot_general x19, matrix products, dot(): lax.dot_general(left, right, ((left_dims, right_dims), ((), ())), preferr...  61.3 us
    all_to_all x4, waiting for transfers between devices, exchange(): lax.all_to_all(value.reshape(cores * experts, per_core, width_dev), ('dp'...  57.4 us
    all_to_all x4, starting transfers between devices, exchange(): lax.all_to_all(value.reshape(cores * experts, per_core, width_dev), ('dp'...  29.4 us
    unnamed x45, local copies, waits for them, and re-layouts  6.28 us
    select_n x3, other arithmetic, in_order(): second = jnp.where(core == 0, other, mine)  5.36 us
    select_n x2, other arithmetic, in_order(): first = jnp.where(core == 0, mine, other)  4.81 us
    ppermute x8, starting transfers between devices, swap(): return lax.ppermute(value, 'dp', [(0, 1), (1, 0)])  4.38 us
  transfers between devices with their start and end apart: 12, of which 4 were waited for; matrix products, arithmetic and copies ran while one was open for 32% of the time, Pallas kernels for 0%

commit v1 on v0

--- a/solution.py
+++ b/solution.py
@@ -2,6 +2,7 @@
 import jax.numpy as jnp
 from jax import lax
 from jax.sharding import PartitionSpec as P
+
 
 F32 = jnp.float32
 BF16 = jnp.bfloat16
@@ -20,7 +21,6 @@
     cores = lax.axis_size("dp")
     core = lax.axis_index("dp")
     hidden_dev = w_gate.shape[2]
-    width = w_gate.shape[1]
     per_core = 8
     core_slots = experts * per_core
     slot_count = cores * core_slots
@@ -37,7 +37,7 @@
             tiled=True,
         ).reshape(cores, core_slots, width_dev)
 
-    def in_order(mine, other, axis):
+    def in_order(mine, other):
         first = jnp.where(core == 0, mine, other)
         second = jnp.where(core == 0, other, mine)
         return first, second
@@ -67,10 +67,10 @@
     sent_grads = (dot(select, out_grad, (1,), (0,)) * slot_probs).astype(BF16)
     grads = exchange(sent_grads)
 
-    gate_lo, gate_hi = in_order(w_gate[0], swap(w_gate[0]), 1)
-    up_lo, up_hi = in_order(w_up[0], swap(w_up[0]), 1)
+    gate_lo, gate_hi = in_order(w_gate[0], swap(w_gate[0]))
+    up_lo, up_hi = in_order(w_up[0], swap(w_up[0]))
     pair_weights = jnp.concatenate([gate_lo, gate_hi, up_lo, up_hi], axis=1)
-    down_weights = jnp.stack(in_order(w_down[0], swap(w_down[0]), 1), axis=0)
+    down_weights = jnp.stack(in_order(w_down[0], swap(w_down[0])), axis=0)
     hidden_all = cores * hidden_dev
 
     rows_full = jnp.concatenate([rows[0], rows[1]], axis=1)
@@ -79,6 +79,10 @@
     up_pre = projected[:, hidden_all:]
     sigma = jax.nn.sigmoid(gate_pre)
     hidden = (gate_pre * sigma * up_pre).astype(BF16)
+    projected, hidden = lax.optimization_barrier((projected, hidden))
+    gate_pre = projected[:, :hidden_all]
+    up_pre = projected[:, hidden_all:]
+    sigma = jax.nn.sigmoid(gate_pre)
     expert_out = jnp.stack(
         [dot(hidden, down_weights[i], (1,), (0,)).astype(BF16) for i in range(cores)], axis=0
     )
@@ -101,14 +105,14 @@
 
     rows_other = swap(rows_full)
     hidden_other = swap(hidden)
-    grads_mine, grads_send = in_order(grads[0], grads[1], 1)
+    grads_mine, grads_send = in_order(grads[0], grads[1])
     grads_other = swap(grads_send)
     down_grad = (
         dot(hidden, grads_mine, (0,), (0,)) + dot(hidden_other, grads_other, (0,), (0,))
     ).astype(BF16)
 
     def share(value):
-        return in_order(value[:, :hidden_dev], value[:, hidden_dev:], 1)
+        return in_order(value[:, :hidden_dev], value[:, hidden_dev:])
 
     gate_mine, gate_send = share(gate_grad)
     up_mine, up_send = share(up_grad)
@@ -149,4 +153,5 @@
         P("expert", None, "dp"),
         P("expert", None, "dp"),
     )
+
     return jax.shard_map(body, mesh=mesh, in_specs=in_specs, out_specs=out_specs, check_vma=False)

time: 181 us -> 188 us (1.039)
  waiting for transfers between devices: 57.4 us -> 71.2 us
  matrix products: 61.3 us -> 56.4 us
  local copies, waits for them, and re-layouts: 8.5 us -> 5.65 us
    all_to_all x4, waiting for transfers between devices: 57.4 us -> 71.1 us  [exchange(): lax.all_to_all(value.reshape(cores * experts, per_core, width_dev), ('dp'...]
    dot_general x19, matrix products: 61.3 us -> 56.4 us  [dot(): lax.dot_general(left, right, ((left_dims, right_dims), ((), ())), preferr...]
    unnamed x45 -> x49, local copies, waits for them, and re-layouts: 6.28 us -> 3.58 us
  transfers between devices with their start and end apart: 12 -> 12, of which waited for: 4 -> 4; matrix products, arithmetic and copies ran while one was open for 32% -> 37% of each run, Pallas kernels for 0% -> 0%
where the time goes in v1:
time: 188 us; the launch traced here: 187 us
  waiting for transfers between devices  71.2 us (38%)
  matrix products  56.4 us (30%)
  starting transfers between devices  34.6 us (18%)
  other arithmetic  18.1 us (10%)
  local copies, waits for them, and re-layouts  5.65 us (3%)
    all_to_all x4, waiting for transfers between devices, exchange(): lax.all_to_all(value.reshape(cores * experts, per_core, width_dev), ('dp'...  71.1 us
    dot_general x19, matrix products, dot(): lax.dot_general(left, right, ((left_dims, right_dims), ((), ())), preferr...  56.4 us
    all_to_all x4, starting transfers between devices, exchange(): lax.all_to_all(value.reshape(cores * experts, per_core, width_dev), ('dp'...  29.5 us
    select_n x3, other arithmetic, in_order(): second = jnp.where(core == 0, other, mine)  5.41 us
    ppermute x8, starting transfers between devices, swap(): return lax.ppermute(value, 'dp', [(0, 1), (1, 0)])  5.09 us
    select_n x2, other arithmetic, in_order(): first = jnp.where(core == 0, mine, other)  4.27 us
  transfers between devices with their start and end apart: 12, of which 4 were waited for; matrix products, arithmetic and copies ran while one was open for 37% of the time, Pallas kernels for 0%

profile of v1, /device:TPU:1, one launch (start us, length us, event | category | flops | bytes accessed | tf_op | source)
XLA Modules:
  0.0 187.0 jit_solution(3974783678755312613)
XLA Ops:
  2.8 2.2 %convert_bitcast_fusion = bf16[128,8,1024]{2,1,0:T(8,128)(2,1)} fusion(bf16[160,1024]{1,0:T(8,128)(2,1)S(1)} %copy-done, s32[160]{0:T(256)S(1)} %bitcast.112, s32[160]{0:T(256)S(1)} %bitcast.107), kind=kOutput, calls=%fused_computation.26 | convolution fusion | flops 337084416 | bytes 2426112 | tf_op jit(solution)/shard_map/dot_general | solution.py:12
  5.1 11.5 %all-to-all-start = ((bf16[128,8,1024]{2,1,0:T(8,128)(2,1)}), bf16[128,8,1024]{2,1,0:T(8,128)(2,1)S(1)}, u32[]{:S(2)}, u32[]{:S(2)}) async-start(bf16[128,8,1024]{2,1,0:T(8,128)(2,1)} %convert_bitcast_fusion), calls=%async_computation | async-start | bytes 4194304 | tf_op jit(solution)/shard_map/all_to_all | solution.py:32
  16.8 2.2 %fusion.14 = bf16[128,8,1024]{2,1,0:T(8,128)(2,1)} fusion(f32[1024]{0:T(1024)S(1)} %add.54, bf16[160,1024]{1,0:T(8,128)(2,1)S(1)} %copy-done.20, s32[160]{0:T(256)S(1)} %bitcast.114, s32[160]{0:T(256)S(1)} %bitcast.109), kind=kOutput, calls=%fused_computation.34 | convolution fusion | flops 338132992 | bytes 2430208 | tf_op jit(solution)/shard_map/dot_general | solution.py:12
  19.1 26.2 %all-to-all-done = bf16[128,8,1024]{2,1,0:T(8,128)(2,1)S(1)} async-done(((bf16[128,8,1024]{2,1,0:T(8,128)(2,1)}), bf16[128,8,1024]{2,1,0:T(8,128)(2,1)S(1)}, u32[]{:S(2)}, u32[]{:S(2)}) %all-to-all-start) | async-done | bytes 2097184 | tf_op jit(solution)/shard_map/all_to_all | solution.py:32
  46.5 6.0 %all-to-all-start.2 = ((bf16[128,8,1024]{2,1,0:T(8,128)(2,1)}), bf16[128,8,1024]{2,1,0:T(8,128)(2,1)S(1)}, u32[]{:S(2)}, u32[]{:S(2)}) async-start(bf16[128,8,1024]{2,1,0:T(8,128)(2,1)} %fusion.14), calls=%async_computation.2 | async-start | bytes 4194304 | tf_op jit(solution)/shard_map/all_to_all | solution.py:32
  54.2 1.7 slice_bitcast_fusion.3
  55.9 1.6 pad_maximum_fusion.1
  57.6 23.6 %all-to-all-done.2 = bf16[128,8,1024]{2,1,0:T(8,128)(2,1)S(1)} async-done(((bf16[128,8,1024]{2,1,0:T(8,128)(2,1)}), bf16[128,8,1024]{2,1,0:T(8,128)(2,1)S(1)}, u32[]{:S(2)}, u32[]{:S(2)}) %all-to-all-start.2) | async-done | bytes 2097184 | tf_op jit(solution)/shard_map/all_to_all | solution.py:32
  83.9 2.1 %broadcast_select_fusion.3 = (bf16[2048,512]{1,0:T(8,128)(2,1)S(1)}, bf16[2048,512]{1,0:T(8,128)(2,1)S(1)}) fusion(bf16[2048,512]{1,0:T(8,128)(2,1)} %collective-permute-done.1, pred[]{:T(512)S(6)} %eq.73, bf16[1,2048,512]{2,1,0:T(8,128)(2,1)S(1)} %copy-done.12), kind=kLoop, calls=%fused_computation.30 | loop fusion | flops 2097152 | bytes 8388609 | tf_op jit(solution)/shard_map/jit(_where)/select_n | solution.py:41
  86.1 2.1 %broadcast_select_fusion.5 = (bf16[2048,512]{1,0:T(8,128)(2,1)S(1)}, bf16[2048,512]{1,0:T(8,128)(2,1)S(1)}) fusion(bf16[2048,512]{1,0:T(8,128)(2,1)} %collective-permute-done, pred[]{:T(512)S(6)} %eq.73, bf16[1,2048,512]{2,1,0:T(8,128)(2,1)S(1)} %copy-done.13), kind=kLoop, calls=%fused_computation.32 | loop fusion | flops 2097152 | bytes 8388609 | tf_op jit(solution)/shard_map/jit(_where)/select_n | solution.py:41
  89.5 4.6 %fusion.81 = f32[512,2048]{1,0:T(8,128)S(1)} fusion(bf16[2048,2048]{1,0:T(8,128)(2,1)S(1)} %pad_maximum_fusion, bf16[512,1024]{1,0:T(8,128)(2,1)S(1)} %copy-done.9, bf16[512,1024]{1,0:T(8,128)(2,1)S(1)} %get-tuple-element.15), kind=kOutput, calls=%fused_computation.103 | convolution fusion | flops 4299161600 | bytes 14680064 | tf_op jit(solution)/shard_map/dot_general | solution.py:12
  94.1 1.6 fusion.6
  97.7 2.5 %fusion.28 = bf16[1,512,1024]{2,1,0:T(8,128)(2,1)S(1)} fusion(bf16[512,1024]{1,0:T(8,128)(2,1)} %fusion.6, bf16[1024,1024]{1,0:T(8,128)(2,1)} %collective-permute-done.2, pred[]{:T(512)S(6)} %eq.73, bf16[1,1024,1024]{2,1,0:T(8,128)(2,1)S(1)} %copy-done.18), kind=kOutput, calls=%fused_computation.43 | convolution fusion | flops 1075314688 | bytes 6291457 | tf_op jit(solution)/shard_map/dot_general | solution.py:12
  100.2 3.2 %fusion.27 = bf16[1,512,1024]{2,1,0:T(8,128)(2,1)S(1)} fusion(bf16[512,1024]{1,0:T(8,128)(2,1)} %fusion.6, bf16[1024,1024]{1,0:T(8,128)(2,1)} %collective-permute-done.2, pred[]{:T(512)S(6)} %eq.73, bf16[1,1024,1024]{2,1,0:T(8,128)(2,1)S(1)} %copy-done.18), kind=kOutput, calls=%fused_computation.42 | convolution fusion | flops 1075314688 | bytes 6291457 | tf_op jit(solution)/shard_map/dot_general | solution.py:12
  103.4 1.5 pad_maximum_fusion.2
  104.9 5.6 %all-to-all-start.1 = ((bf16[128,8,1024]{2,1,0:T(8,128)(2,1)}), bf16[128,8,1024]{2,1,0:T(8,128)(2,1)S(1)}, u32[]{:S(2)}, u32[]{:S(2)}) async-start(bf16[128,8,1024]{2,1,0:T(8,128)(2,1)} %bitcast.104), calls=%async_computation.1 | async-start | bytes 4194304 | tf_op jit(solution)/shard_map/all_to_all | solution.py:32
  110.5 3.4 %fusion.48 = f32[512,1024]{1,0:T(8,128)S(1)} fusion(bf16[128,8,1024]{2,1,0:T(8,128)(2,1)} %copy-done.3, bf16[1024,1024]{1,0:T(8,128)(2,1)} %collective-permute-done.2, pred[]{:T(512)S(6)} %eq.73, bf16[1,1024,1024]{2,1,0:T(8,128)(2,1)} %param.13), kind=kOutput, calls=%fused_computation.59 | convolution fusion | flops 1074790400 | bytes 7340033 | tf_op jit(solution)/shard_map/dot_general | solution.py:12
  113.9 5.0 %multiply_convert_fusion.2 = (bf16[512,1024]{1,0:T(8,128)(2,1)S(1)}, bf16[512,1024]{1,0:T(8,128)(2,1)S(1)}) fusion(f32[512,2048]{1,0:T(8,128)} %copy-done.7, f32[512,1024]{1,0:T(8,128)S(1)} %fusion.48, bf16[1024,1024]{1,0:T(8,128)(2,1)} %collective-permute-done.2, pred[]{:T(512)S(6)} %eq.73, bf16[1,1024,1024]{2,1,0:T(8,128)(2,1)S(1)} %copy-done.19, ...), kind=kOutput, calls=%fused_computation.24 | convolution fusion | flops 1082130432 | bytes 13631489 | tf_op jit(solution)/shard_map/dot_general | solution.py:12
  119.0 2.4 %fusion.21 = bf16[1,512,1024]{2,1,0:T(8,128)(2,1)S(1)} fusion(bf16[2048,2048]{1,0:T(8,128)(2,1)S(1)} %bitcast.102, bf16[512,1024]{1,0:T(8,128)(2,1)S(1)} %get-tuple-element.10, bf16[512,1024]{1,0:T(8,128)(2,1)S(1)} %get-tuple-element.9), kind=kOutput, calls=%fused_computation.40 | convolution fusion | flops 2152202240 | bytes 7340032 | tf_op jit(solution)/shard_map/dot_general | solution.py:12
  121.4 2.4 %fusion.24 = bf16[1,512,1024]{2,1,0:T(8,128)(2,1)S(1)} fusion(bf16[2048,2048]{1,0:T(8,128)(2,1)S(1)} %bitcast.102, bf16[512,1024]{1,0:T(8,128)(2,1)S(1)} %get-tuple-element.10, bf16[512,1024]{1,0:T(8,128)(2,1)S(1)} %get-tuple-element.9), kind=kOutput, calls=%fused_computation.41 | convolution fusion | flops 2152202240 | bytes 7340032 | tf_op jit(solution)/shard_map/dot_general | solution.py:12
  125.3 3.3 %fusion.52 = f32[2048,512]{1,0:T(8,128)} fusion(pred[]{:T(512)S(6)} %eq.73, bf16[512,1024]{1,0:T(8,128)(2,1)S(1)} %get-tuple-element.9, bf16[512,1024]{1,0:T(8,128)(2,1)S(1)} %copy-done.10, bf16[512,1024]{1,0:T(8,128)(2,1)S(1)} %get-tuple-element.15), kind=kOutput, calls=%fused_computation.67 | convolution fusion | flops 1078198272 | bytes 7340033 | tf_op jit(solution)/shard_map/dot_general | solution.py:12
  128.6 10.6 %all-to-all-done.1 = bf16[128,8,1024]{2,1,0:T(8,128)(2,1)S(1)} async-done(((bf16[128,8,1024]{2,1,0:T(8,128)(2,1)}), bf16[128,8,1024]{2,1,0:T(8,128)(2,1)S(1)}, u32[]{:S(2)}, u32[]{:S(2)}) %all-to-all-start.1) | async-done | bytes 2097184 | tf_op jit(solution)/shard_map/all_to_all | solution.py:32
  139.1 6.5 %all-to-all-start.3 = ((bf16[128,8,1024]{2,1,0:T(8,128)(2,1)}), bf16[128,8,1024]{2,1,0:T(8,128)(2,1)}, u32[]{:S(2)}, u32[]{:S(2)}) async-start(bf16[128,8,1024]{2,1,0:T(8,128)(2,1)} %bitcast.103), calls=%async_computation.3 | async-start | bytes 4194304 | tf_op jit(solution)/shard_map/all_to_all | solution.py:32
  145.6 2.2 %broadcast_select_fusion.12 = bf16[512,512]{1,0:T(8,128)(2,1)} fusion(pred[]{:T(512)S(6)} %eq.73, bf16[512,1024]{1,0:T(8,128)(2,1)} %copy-done.16), kind=kLoop, calls=%fused_computation.71 | loop fusion | flops 262144 | bytes 1572865 | tf_op jit(solution)/shard_map/jit(_where)/select_n | solution.py:42
  147.8 2.1 %broadcast_select_fusion.11 = bf16[512,512]{1,0:T(8,128)(2,1)} fusion(pred[]{:T(512)S(6)} %eq.73, bf16[512,1024]{1,0:T(8,128)(2,1)} %copy-done.14), kind=kLoop, calls=%fused_computation.69 | loop fusion | flops 262144 | bytes 1572865 | tf_op jit(solution)/shard_map/jit(_where)/select_n | solution.py:42
  151.1 3.4 %fusion.50 = f32[2048,512]{1,0:T(8,128)} fusion(pred[]{:T(512)S(6)} %eq.73, bf16[512,1024]{1,0:T(8,128)(2,1)S(1)} %copy-done.15, bf16[512,1024]{1,0:T(8,128)(2,1)S(1)} %copy-done.11, bf16[512,1024]{1,0:T(8,128)(2,1)S(1)} %get-tuple-element.15), kind=kOutput, calls=%fused_computation.65 | convolution fusion | flops 1078198272 | bytes 7340033 | tf_op jit(solution)/shard_map/dot_general | solution.py:12
  154.4 2.5 %fusion.45 = f32[1024,1024]{1,0:T(8,128)S(1)} fusion(bf16[512,1024]{1,0:T(8,128)(2,1)} %fusion.6, pred[]{:T(512)S(6)} %eq.73, bf16[128,8,1024]{2,1,0:T(8,128)(2,1)S(1)} %copy-done.5), kind=kOutput, calls=%fused_computation.55 | convolution fusion | flops 1074266112 | bytes 7340033 | tf_op jit(solution)/shard_map/dot_general | solution.py:12
  157.0 4.2 %fusion.13 = bf16[1,1024,1024]{2,1,0:T(8,128)(2,1)} fusion(f32[1024,1024]{1,0:T(8,128)S(1)} %fusion.45, bf16[512,1024]{1,0:T(8,128)(2,1)} %collective-permute-done.6, bf16[512,1024]{1,0:T(8,128)(2,1)} %collective-permute-done.7), kind=kOutput, calls=%fused_computation.33 | convolution fusion | flops 1075838976 | bytes 8388608 | tf_op jit(solution)/shard_map/dot_general | solution.py:12
  163.1 10.9 %all-to-all-done.3 = bf16[128,8,1024]{2,1,0:T(8,128)(2,1)} async-done(((bf16[128,8,1024]{2,1,0:T(8,128)(2,1)}), bf16[128,8,1024]{2,1,0:T(8,128)(2,1)}, u32[]{:S(2)}, u32[]{:S(2)}) %all-to-all-start.3) | async-done | bytes 2097184 | tf_op jit(solution)/shard_map/all_to_all | solution.py:32
  173.9 2.9 %fusion.41 = bf16[160,1024]{1,0:T(8,128)(2,1)} fusion(bf16[128,8,1024]{2,1,0:T(8,128)(2,1)} %all-to-all-done.3, s32[160]{0:T(256)S(1)} %bitcast.116, s32[160]{0:T(256)S(1)} %bitcast.111), kind=kOutput, calls=%fused_computation.48 | convolution fusion | flops 336199680 | bytes 2426112 | tf_op jit(solution)/shard_map/dot_general | solution.py:12
  176.8 5.7 %fusion.4 = bf16[1,2048,512]{2,1,0:T(8,128)(2,1)} fusion(f32[2048,512]{1,0:T(8,128)} %fusion.52, bf16[512,2048]{1,0:T(8,128)(2,1)} %collective-permute-done.3, bf16[512,512]{1,0:T(8,128)(2,1)} %collective-permute-done.4), kind=kOutput, calls=%fused_computation.9 | convolution fusion | flops 1075838976 | bytes 8912896 | tf_op jit(solution)/shard_map/dot_general | solution.py:12
  182.6 4.4 %fusion.5 = bf16[1,2048,512]{2,1,0:T(8,128)(2,1)} fusion(f32[2048,512]{1,0:T(8,128)S(1)} %copy-done.21, bf16[512,2048]{1,0:T(8,128)(2,1)} %collective-permute-done.3, bf16[512,512]{1,0:T(8,128)(2,1)} %collective-permute-done.5), kind=kOutput, calls=%fused_computation.10 | convolution fusion | flops 1075838976 | bytes 8912896 | tf_op jit(solution)/shard_map/dot_general | solution.py:12
  (81 shorter events, 15.9 us)
Async XLA Ops:
  0.6 2.2 %copy-start = (bf16[160,1024]{1,0:T(8,128)(2,1)S(1)}, bf16[160,1024]{1,0:T(8,128)(2,1)}, u32[]{:S(2)}) copy-start(bf16[160,1024]{1,0:T(8,128)(2,1)} %param.7) | copy-start | bytes 983044
  5.1 11.5 %copy-start.17 = (f32[160,2]{0,1:T(2,128)S(1)}, f32[160,2]{0,1:T(2,128)}, u32[]{:S(2)}) copy-start(f32[160,2]{0,1:T(2,128)} %param.9) | copy-start | bytes 3844
  5.1 11.8 %copy-start.20 = (bf16[160,1024]{1,0:T(8,128)(2,1)S(1)}, bf16[160,1024]{1,0:T(8,128)(2,1)}, u32[]{:S(2)}) copy-start(bf16[160,1024]{1,0:T(8,128)(2,1)} %param.10) | copy-start | bytes 983044
  5.1 40.2 %all-to-all-start = ((bf16[128,8,1024]{2,1,0:T(8,128)(2,1)}), bf16[128,8,1024]{2,1,0:T(8,128)(2,1)S(1)}, u32[]{:S(2)}, u32[]{:S(2)}) async-start(bf16[128,8,1024]{2,1,0:T(8,128)(2,1)} %convert_bitcast_fusion), calls=%async_computation | async-start | bytes 4194304 | tf_op jit(solution)/shard_map/all_to_all | solution.py:32
  46.5 34.7 %all-to-all-start.2 = ((bf16[128,8,1024]{2,1,0:T(8,128)(2,1)}), bf16[128,8,1024]{2,1,0:T(8,128)(2,1)S(1)}, u32[]{:S(2)}, u32[]{:S(2)}) async-start(bf16[128,8,1024]{2,1,0:T(8,128)(2,1)} %fusion.14), calls=%async_computation.2 | async-start | bytes 4194304 | tf_op jit(solution)/shard_map/all_to_all | solution.py:32
  52.5 30.9 %collective-permute-start.1 = (bf16[2048,512]{1,0:T(8,128)(2,1)}, bf16[2048,512]{1,0:T(8,128)(2,1)}, u32[]{:S(2)}, u32[]{:S(2)}) collective-permute-start(bf16[2048,512]{1,0:T(8,128)(2,1)} %bitcast.105), channel_id=1, source_target_pairs={{0,64},{64,0},{1,65},{65,1},{2,66},{66,2},{3,67},{67,3},{4,68},{68... | collective-permute-start | bytes 6291464 | tf_op jit(solution)/shard_map/ppermute | solution.py:29
  53.7 32.4 %collective-permute-start = (bf16[2048,512]{1,0:T(8,128)(2,1)}, bf16[2048,512]{1,0:T(8,128)(2,1)}, u32[]{:S(2)}, u32[]{:S(2)}) collective-permute-start(bf16[2048,512]{1,0:T(8,128)(2,1)} %bitcast.106), channel_id=1, source_target_pairs={{0,64},{64,0},{1,65},{65,1},{2,66},{66,2},{3,67},{67,3},{4,68},{68... | collective-permute-start | bytes 6291464 | tf_op jit(solution)/shard_map/ppermute | solution.py:29
  53.8 43.9 %collective-permute-start.2 = (bf16[1024,1024]{1,0:T(8,128)(2,1)}, bf16[1024,1024]{1,0:T(8,128)(2,1)}, u32[]{:S(2)}, u32[]{:S(2)}) collective-permute-start(bf16[1024,1024]{1,0:T(8,128)(2,1)} %bitcast.121), channel_id=1, source_target_pairs={{0,64},{64,0},{1,65},{65,1},{2,66},{66,2},{3,67},{67,3},{4,68},{68... | collective-permute-start | bytes 6291464 | tf_op jit(solution)/shard_map/ppermute | solution.py:29
  57.6 119.3 %collective-permute-start.3 = (bf16[512,2048]{1,0:T(8,128)(2,1)}, bf16[512,2048]{1,0:T(8,128)(2,1)}, u32[]{:S(2)}, u32[]{:S(2)}) collective-permute-start(bf16[512,2048]{1,0:T(8,128)(2,1)} %pad_maximum_fusion.1), channel_id=1, source_target_pairs={{0,64},{64,0},{1,65},{65,1},{2,66},{66,2},{3,67},{67,3},{4,68},{68... | collective-permute-start | bytes 6291464 | tf_op jit(solution)/shard_map/ppermute | solution.py:29
  81.2 4.9 %copy-start.3 = (bf16[128,8,1024]{2,1,0:T(8,128)(2,1)}, bf16[128,8,1024]{2,1,0:T(8,128)(2,1)S(1)}, u32[]{:S(2)}) copy-start(bf16[128,8,1024]{2,1,0:T(8,128)(2,1)S(1)} %all-to-all-done.2) | copy-start | bytes 6291460
  81.2 2.7 %copy-start.12 = (bf16[1,2048,512]{2,1,0:T(8,128)(2,1)S(1)}, bf16[1,2048,512]{2,1,0:T(8,128)(2,1)}, u32[]{:S(2)}) copy-start(bf16[1,2048,512]{2,1,0:T(8,128)(2,1)} %param.12) | copy-start | bytes 6291460
  82.4 3.7 %copy-start.13 = (bf16[1,2048,512]{2,1,0:T(8,128)(2,1)S(1)}, bf16[1,2048,512]{2,1,0:T(8,128)(2,1)}, u32[]{:S(2)}) copy-start(bf16[1,2048,512]{2,1,0:T(8,128)(2,1)} %param.11) | copy-start | bytes 6291460
  82.4 74.6 %collective-permute-start.7 = (bf16[512,1024]{1,0:T(8,128)(2,1)}, bf16[512,1024]{1,0:T(8,128)(2,1)}, u32[]{:S(2)}, u32[]{:S(2)}) collective-permute-start(bf16[512,1024]{1,0:T(8,128)(2,1)} %broadcast_select_fusion.6), channel_id=1, source_target_pairs={{0,64},{64,0},{1,65},{65,1},{2,66},{66,2},{3,67},{67,3},{4,68},{68... | collective-permute-start | bytes 3145736 | tf_op jit(solution)/shard_map/ppermute | solution.py:29
  89.5 4.6 %copy-start.2 = (bf16[2048,2048]{1,0:T(8,128)(2,1)}, bf16[2048,2048]{1,0:T(8,128)(2,1)S(1)}, u32[]{:S(2)}) copy-start(bf16[2048,2048]{1,0:T(8,128)(2,1)S(1)} %pad_maximum_fusion) | copy-start | bytes 25165828
  94.1 2.5 %copy-start.7 = (f32[512,2048]{1,0:T(8,128)}, f32[512,2048]{1,0:T(8,128)S(1)}, u32[]{:S(2)}) copy-start(f32[512,2048]{1,0:T(8,128)S(1)} %fusion.81) | copy-start | bytes 12582916
  94.1 3.6 %copy-start.18 = (bf16[1,1024,1024]{2,1,0:T(8,128)(2,1)S(1)}, bf16[1,1024,1024]{2,1,0:T(8,128)(2,1)}, u32[]{:S(2)}) copy-start(bf16[1,1024,1024]{2,1,0:T(8,128)(2,1)} %param.13) | copy-start | bytes 6291460
  96.6 60.4 %collective-permute-start.6 = (bf16[512,1024]{1,0:T(8,128)(2,1)}, bf16[512,1024]{1,0:T(8,128)(2,1)}, u32[]{:S(2)}, u32[]{:S(2)}) collective-permute-start(bf16[512,1024]{1,0:T(8,128)(2,1)} %fusion.6), channel_id=1, source_target_pairs={{0,64},{64,0},{1,65},{65,1},{2,66},{66,2},{3,67},{67,3},{4,68},{68... | collective-permute-start | bytes 3145736 | tf_op jit(solution)/shard_map/ppermute | solution.py:29
  104.9 34.2 %all-to-all-start.1 = ((bf16[128,8,1024]{2,1,0:T(8,128)(2,1)}), bf16[128,8,1024]{2,1,0:T(8,128)(2,1)S(1)}, u32[]{:S(2)}, u32[]{:S(2)}) async-start(bf16[128,8,1024]{2,1,0:T(8,128)(2,1)} %bitcast.104), calls=%async_computation.1 | async-start | bytes 4194304 | tf_op jit(solution)/shard_map/all_to_all | solution.py:32
  110.5 3.4 %copy-start.4 = (bf16[128,8,1024]{2,1,0:T(8,128)(2,1)S(1)}, bf16[128,8,1024]{2,1,0:T(8,128)(2,1)}, u32[]{:S(2)}) copy-start(bf16[128,8,1024]{2,1,0:T(8,128)(2,1)} %copy-done.3) | copy-start | bytes 6291460
  110.5 3.4 %copy-start.19 = (bf16[1,1024,1024]{2,1,0:T(8,128)(2,1)S(1)}, bf16[1,1024,1024]{2,1,0:T(8,128)(2,1)}, u32[]{:S(2)}) copy-start(bf16[1,1024,1024]{2,1,0:T(8,128)(2,1)} %param.13) | copy-start | bytes 6291460
  110.5 8.4 %slice-start = ((s8[8388608]{0:T(1024)(128)(4,1)}), s8[4194304]{0:T(1024)(128)(4,1)S(1)}, s32[]{:S(2)}) async-start(s8[8388608]{0:T(1024)(128)(4,1)} %bitcast.101), calls=%async_computation.4 | async-start | bytes 8388608
  113.9 5.0 %slice-start.1 = ((s8[8388608]{0:T(1024)(128)(4,1)}), s8[4194304]{0:T(1024)(128)(4,1)S(1)}, s32[]{:S(2)}) async-start(s8[8388608]{0:T(1024)(128)(4,1)} %bitcast.101), calls=%async_computation.5 | async-start | bytes 8388608
  118.9 2.4 %copy-start.14 = (bf16[512,1024]{1,0:T(8,128)(2,1)}, bf16[512,1024]{1,0:T(8,128)(2,1)S(1)}, u32[]{:S(2)}) copy-start(bf16[512,1024]{1,0:T(8,128)(2,1)S(1)} %get-tuple-element.10) | copy-start | bytes 3145732
  118.9 6.3 %copy-start.16 = (bf16[512,1024]{1,0:T(8,128)(2,1)}, bf16[512,1024]{1,0:T(8,128)(2,1)S(1)}, u32[]{:S(2)}) copy-start(bf16[512,1024]{1,0:T(8,128)(2,1)S(1)} %get-tuple-element.9) | copy-start | bytes 3145732
  139.1 34.8 %all-to-all-start.3 = ((bf16[128,8,1024]{2,1,0:T(8,128)(2,1)}), bf16[128,8,1024]{2,1,0:T(8,128)(2,1)}, u32[]{:S(2)}, u32[]{:S(2)}) async-start(bf16[128,8,1024]{2,1,0:T(8,128)(2,1)} %bitcast.103), calls=%async_computation.3 | async-start | bytes 4194304 | tf_op jit(solution)/shard_map/all_to_all | solution.py:32
  145.6 5.4 %copy-start.11 = (bf16[512,1024]{1,0:T(8,128)(2,1)S(1)}, bf16[512,1024]{1,0:T(8,128)(2,1)}, u32[]{:S(2)}) copy-start(bf16[512,1024]{1,0:T(8,128)(2,1)} %copy-done.8) | copy-start | bytes 3145732
  145.6 5.4 %copy-start.15 = (bf16[512,1024]{1,0:T(8,128)(2,1)S(1)}, bf16[512,1024]{1,0:T(8,128)(2,1)}, u32[]{:S(2)}) copy-start(bf16[512,1024]{1,0:T(8,128)(2,1)} %copy-done.14) | copy-start | bytes 3145732
  149.9 4.5 %copy-start.5 = (bf16[128,8,1024]{2,1,0:T(8,128)(2,1)S(1)}, bf16[128,8,1024]{2,1,0:T(8,128)(2,1)}, u32[]{:S(2)}) copy-start(bf16[128,8,1024]{2,1,0:T(8,128)(2,1)} %copy-done.3) | copy-start | bytes 6291460
  149.9 26.9 %collective-permute-start.4 = (bf16[512,512]{1,0:T(8,128)(2,1)}, bf16[512,512]{1,0:T(8,128)(2,1)}, u32[]{:S(2)}, u32[]{:S(2)}) collective-permute-start(bf16[512,512]{1,0:T(8,128)(2,1)} %broadcast_select_fusion.12), channel_id=1, source_target_pairs={{0,64},{64,0},{1,65},{65,1},{2,66},{66,2},{3,67},{67,3},{4,68},{68... | collective-permute-start | bytes 1572872 | tf_op jit(solution)/shard_map/ppermute | solution.py:29
  151.1 31.5 %collective-permute-start.5 = (bf16[512,512]{1,0:T(8,128)(2,1)}, bf16[512,512]{1,0:T(8,128)(2,1)}, u32[]{:S(2)}, u32[]{:S(2)}) collective-permute-start(bf16[512,512]{1,0:T(8,128)(2,1)} %broadcast_select_fusion.11), channel_id=1, source_target_pairs={{0,64},{64,0},{1,65},{65,1},{2,66},{66,2},{3,67},{67,3},{4,68},{68... | collective-permute-start | bytes 1572872 | tf_op jit(solution)/shard_map/ppermute | solution.py:29
  176.8 5.8 %copy-start.21 = (f32[2048,512]{1,0:T(8,128)S(1)}, f32[2048,512]{1,0:T(8,128)}, u32[]{:S(2)}) copy-start(f32[2048,512]{1,0:T(8,128)} %fusion.50) | copy-start | bytes 12582916
  182.6 4.4 %copy-start.1 = (bf16[160,1024]{1,0:T(8,128)(2,1)S(1)}, bf16[160,1024]{1,0:T(8,128)(2,1)}, u32[]{:S(2)}) copy-start(bf16[160,1024]{1,0:T(8,128)(2,1)} %param.7) | copy-start | bytes 983044
  (4 other events, 5.7 us)

commit v2 on v0

v2 whole, which is shorter than its diff:
```python
import functools

import jax
import jax.numpy as jnp
from jax import lax
from jax.experimental import pallas as pl
from jax.experimental.pallas import tpu as pltpu
from jax.sharding import PartitionSpec as P


F32 = jnp.float32
BF16 = jnp.bfloat16
I32 = jnp.int32
SUB = 8
BLOCKS = 4
HBM = pl.BlockSpec(memory_space=pl.ANY)
VMEM = pl.BlockSpec(memory_space=pltpu.VMEM)


def dot(left, right, left_dims, right_dims):
    return lax.dot_general(
        left, right, ((left_dims, right_dims), ((), ())), preferred_element_type=F32
    )


def mm(left, right):
    return dot(left, right, (1,), (0,))


def one_hot(hits):
    return jnp.where(hits, 1.0, 0.0).astype(BF16)


def slots_of(ids, axis, experts):
    tok = ids[0].shape[1 - axis]
    shape = (experts, tok) if axis == 0 else (tok, experts)
    expert = lax.broadcasted_iota(I32, shape, axis)
    named = [ids[k] == expert for k in range(2)]
    either = one_hot(named[0] | named[1])
    row = lax.broadcasted_iota(I32, (tok, tok), axis)
    other = lax.broadcasted_iota(I32, (tok, tok), 1 - axis)
    ahead = one_hot(row < other)
    earlier = mm(either, ahead) if axis == 0 else mm(ahead, either)
    slots = []
    for k in range(2):
        rank = jnp.sum(jnp.where(named[k], earlier, 0.0), axis=axis, keepdims=True).astype(I32)
        slots.append((rank & 1) * (experts * SUB) + ids[k] * SUB + (rank >> 1))
    return slots


def dispatch_kernel(weighted, experts, ids_ref, probs_ref, x_ref, out_ref):
    tok = x_ref.shape[0]
    chunk = out_ref.shape[0] // BLOCKS
    slots = slots_of([ids_ref[k : k + 1, :] for k in range(2)], 0, experts)
    for n in range(BLOCKS):
        spot = lax.broadcasted_iota(I32, (chunk, tok), 0) + n * chunk
        hits = [spot == slots[k] for k in range(2)]
        value = mm(one_hot(hits[0] | hits[1]), x_ref[...])
        if weighted:
            probs = jnp.where(hits[0], probs_ref[0:1, :], 0.0) + jnp.where(
                hits[1], probs_ref[1:2, :], 0.0
            )
            value = value * jnp.sum(probs, axis=1, keepdims=True)
        out_ref[n * chunk : (n + 1) * chunk, :] = value.astype(BF16)


def dispatch(ids_t, probs_t, source, experts, weighted):
    return pl.pallas_call(
        functools.partial(dispatch_kernel, weighted, experts),
        out_shape=jax.ShapeDtypeStruct((2 * experts * SUB, source.shape[1]), BF16),
        in_specs=[VMEM] * 3,
        out_specs=VMEM,
        name="send_grads" if weighted else "send_rows",
    )(ids_t, probs_t, source)


def mix_kernel(ids_ref, probs_ref, back_hbm, out_ref, select_ref, back_ref, sems):
    tok = out_ref.shape[0]
    rows = back_ref.shape[0]
    chunk = rows // BLOCKS
    loads = []
    for n in range(BLOCKS):
        here = pl.ds(n * chunk, chunk)
        loads.append(pltpu.make_async_copy(back_hbm.at[here], back_ref.at[here], sems.at[n]))
        loads[n].start()
    slots = slots_of([ids_ref[:, k : k + 1] for k in range(2)], 1, rows // (2 * SUB))
    sums = [0.0, 0.0]
    for n in range(BLOCKS):
        spot = lax.broadcasted_iota(I32, (tok, chunk), 1) + n * chunk
        hits = [spot == slots[k] for k in range(2)]
        select_ref[:, n * chunk : (n + 1) * chunk] = one_hot(hits[0] | hits[1])
        loads[n].wait()
        part = back_ref[n * chunk : (n + 1) * chunk, :]
        sums = [sums[k] + mm(one_hot(hits[k]), part) for k in range(2)]
    total = sums[0] * probs_ref[:, 0:1] + sums[1] * probs_ref[:, 1:2]
    out_ref[...] = total.astype(BF16)


def mix(ids, probs, back):
    tok = ids.shape[0]
    return pl.pallas_call(
        mix_kernel,
        out_shape=[
            jax.ShapeDtypeStruct((tok, back.shape[1]), BF16),
            jax.ShapeDtypeStruct((tok, back.shape[0]), BF16),
        ],
        in_specs=[VMEM, VMEM, HBM],
        scratch_shapes=[pltpu.VMEM(back.shape, BF16), pltpu.SemaphoreType.DMA((BLOCKS,))],
        name="mix",
    )(ids, probs, back)


def add_kernel(select_ref, back_ref, out_ref):
    out_ref[...] = mm(select_ref[...], back_ref[...]).astype(BF16)


def add_routes(select, back):
    return pl.pallas_call(
        add_kernel,
        out_shape=jax.ShapeDtypeStruct((select.shape[0], back.shape[1]), BF16),
        in_specs=[VMEM, VMEM],
        out_specs=VMEM,
        name="add_routes",
    )(select, back)


def write_halves(value_of, stage_ref, out_hbm, sems):
    copies = []
    for half in range(2):
        stage_ref[half] = value_of(half).astype(BF16)
        copies.append(
            pltpu.make_async_copy(stage_ref.at[half], out_hbm.at[half], sems.at[half])
        )
        copies[half].start()
    for copy in copies:
        copy.wait()


def forward_kernel(
    x_hbm, wg_ref, wu_ref, wd_hbm, gp_ref, up_ref, h_ref, out_hbm,
    x_ref, wd_ref, hidden_ref, stage_ref, x_sem, wd_sem, out_sems,
):
    step = pl.program_id(0)
    block = h_ref.shape[1]
    width = x_ref.shape[2]
    load = pltpu.make_async_copy(wd_hbm, wd_ref, wd_sem)

    @pl.when(step == 0)
    def _():
        fetch = pltpu.make_async_copy(x_hbm, x_ref, x_sem)
        fetch.start()
        load.start()
        fetch.wait()

    def project(w_ref):
        return mm(x_ref[0], w_ref[:width, :]) + mm(x_ref[1], w_ref[width:, :])

    gate_pre = project(wg_ref)
    up_pre = project(wu_ref)
    gp_ref[...] = gate_pre
    up_ref[...] = up_pre
    hidden = (gate_pre * jax.nn.sigmoid(gate_pre) * up_pre).astype(BF16)
    h_ref[...] = hidden
    hidden_ref[:, pl.ds(pl.multiple_of(step * block, block), block)] = hidden

    @pl.when(step == BLOCKS - 1)
    def _():
        load.wait()

        def value_of(half):
            return mm(hidden_ref[...], wd_ref[:, half * width : (half + 1) * width])

        write_halves(value_of, stage_ref, out_hbm, out_sems)


def forward(rows_in, pair_weights, down_weights):
    cores, rows, width = rows_in.shape
    hidden, full = down_weights.shape
    block = hidden // BLOCKS
    cols = pl.BlockSpec((rows, block), lambda i: (0, i))
    return pl.pallas_call(
        forward_kernel,
        grid=(BLOCKS,),
        in_specs=[
            pl.BlockSpec(memory_space=pltpu.HBM),
            pl.BlockSpec((full, block), lambda i: (0, i)),
            pl.BlockSpec((full, block), lambda i: (0, i + BLOCKS)),
            HBM,
        ],
        out_specs=[cols, cols, cols, HBM],
        out_shape=[
            jax.ShapeDtypeStruct((rows, hidden), F32),
            jax.ShapeDtypeStruct((rows, hidden), F32),
            jax.ShapeDtypeStruct((rows, hidden), BF16),
            jax.ShapeDtypeStruct((cores, rows, width), BF16),
        ],
        scratch_shapes=[
            pltpu.VMEM((cores, rows, width), BF16),
            pltpu.VMEM((hidden, full), BF16),
            pltpu.VMEM((rows, hidden), BF16),
            pltpu.VMEM((cores, rows, width), BF16),
            pltpu.SemaphoreType.DMA,
            pltpu.SemaphoreType.DMA,
            pltpu.SemaphoreType.DMA((2,)),
        ],
        name="forward",
    )(rows_in, pair_weights, pair_weights, down_weights)


def backward_kernel(
    g_ref, gp_ref, up_ref, wd_ref, wp_hbm, gg_ref, ug_ref, out_hbm,
    wp_ref, pair_ref, stage_ref, wp_sem, out_sems,
):
    step = pl.program_id(0)
    block = gg_ref.shape[1]
    width = g_ref.shape[2]
    hidden = BLOCKS * block
    load = pltpu.make_async_copy(wp_hbm, wp_ref, wp_sem)

    @pl.when(step == 0)
    def _():
        load.start()

    hidden_grad = dot(g_ref[0], wd_ref[:, :width], (1,), (1,)) + dot(
        g_ref[1], wd_ref[:, width:], (1,), (1,)
    )
    gate_pre = gp_ref[...]
    up_pre = up_ref[...]
    sigma = jax.nn.sigmoid(gate_pre)
    gate_grad = (hidden_grad * up_pre * sigma * (1.0 + gate_pre * (1.0 - sigma))).astype(BF16)
    up_grad = (hidden_grad * gate_pre * sigma).astype(BF16)
    gg_ref[...] = gate_grad
    ug_ref[...] = up_grad
    pair_ref[:, pl.ds(pl.multiple_of(step * block, block), block)] = gate_grad
    pair_ref[:, pl.ds(pl.multiple_of(hidden + step * block, block), block)] = up_grad

    @pl.when(step == BLOCKS - 1)
    def _():
        load.wait()

        def value_of(half):
            return dot(pair_ref[...], wp_ref[half * width : (half + 1) * width, :], (1,), (1,))

        write_halves(value_of, stage_ref, out_hbm, out_sems)


def backward(grads_in, gate_pre, up_pre, pair_weights, down_weights):
    cores, rows, width = grads_in.shape
    hidden, full = down_weights.shape
    block = hidden // BLOCKS
    cols = pl.BlockSpec((rows, block), lambda i: (0, i))
    return pl.pallas_call(
        backward_kernel,
        grid=(BLOCKS,),
        in_specs=[
            pl.BlockSpec((cores, rows, width), lambda i: (0, 0, 0)),
            cols,
            cols,
            pl.BlockSpec((block, full), lambda i: (i, 0)),
            HBM,
        ],
        out_specs=[cols, cols, HBM],
        out_shape=[
            jax.ShapeDtypeStruct((rows, hidden), BF16),
            jax.ShapeDtypeStruct((rows, hidden), BF16),
            jax.ShapeDtypeStruct((cores, rows, width), BF16),
        ],
        scratch_shapes=[
            pltpu.VMEM((full, 2 * hidden), BF16),
            pltpu.VMEM((rows, 2 * hidden), BF16),
            pltpu.VMEM((cores, rows, width), BF16),
            pltpu.SemaphoreType.DMA,
            pltpu.SemaphoreType.DMA((2,)),
        ],
        name="backward",
    )(grads_in, gate_pre, up_pre, down_weights, pair_weights)


def both(mine, other, mine_g, other_g):
    return dot(mine, mine_g, (0,), (0,)) + dot(other, other_g, (0,), (0,))


def pair_grad_kernel(core_ref, x_ref, xp_ref, g_ref, gp_ref, u_ref, up_ref, dg_ref, du_ref):
    dg_ref[...] = both(x_ref[...], xp_ref[...], g_ref[...], gp_ref[...]).astype(BF16)
    du_ref[...] = both(x_ref[...], xp_ref[...], u_ref[...], up_ref[...]).astype(BF16)


def down_grad_kernel(core_ref, h_ref, hp_ref, g_ref, gp_ref, out_ref):
    out_ref[...] = both(h_ref[...], hp_ref[...], g_ref[...], gp_ref[...]).astype(BF16)


def share_call(kernel, core, steps, operands, out_rows, out_cols, outs):
    block = out_rows // steps
    grid_spec = pltpu.PrefetchScalarGridSpec(
        num_scalar_prefetch=1,
        grid=(steps,),
        in_specs=[spec for _, spec in operands],
        out_specs=[pl.BlockSpec((block, out_cols), lambda i, c: (i, 0))] * outs,
    )
    shape = jax.ShapeDtypeStruct((out_rows, out_cols), BF16)
    return pl.pallas_call(kernel, out_shape=[shape] * outs, grid_spec=grid_spec)(
        core, *[value for value, _ in operands]
    )


def pair_grads(core, rows_mine, rows_other, rights):
    cores, rows, width = rows_mine.shape
    half = rights[0].shape[1] // 2
    block = width // 2
    left = pl.BlockSpec((None, rows, block), lambda i, c: (i // 2, 0, i % 2))
    right = pl.BlockSpec((rows, half), lambda i, c: (0, c[0]))
    operands = [(rows_mine, left), (rows_other, left)] + [(value, right) for value in rights]
    return share_call(pair_grad_kernel, core, 2 * cores, operands, cores * width, half, 2)


def down_grads(core, hidden_mine, hidden_other, grads_mine, grads_other):
    _, rows, width = grads_mine.shape
    hidden = hidden_mine.shape[1]
    left = pl.BlockSpec((rows, hidden // 2), lambda i, c: (0, i))
    right = pl.BlockSpec((None, rows, width), lambda i, c: (c[0], 0, 0))
    operands = [
        (hidden_mine, left), (hidden_other, left), (grads_mine, right), (grads_other, right),
    ]
    return share_call(down_grad_kernel, core, 2, operands, hidden, width, 1)[0]


def body(patches, expert_ids, gate_probs, out_grad, w_gate, w_up, w_down):
    width = patches.shape[1]
    experts = lax.axis_size("expert")
    core = lax.axis_index("dp")
    core_id = core.astype(I32)[None]

    def swap(value):
        return lax.ppermute(value, "dp", [(0, 1), (1, 0)])

    def exchange(value):
        return lax.all_to_all(
            value.reshape(2 * experts, SUB, width),
            ("dp", "expert"),
            split_axis=0,
            concat_axis=0,
            tiled=True,
        ).reshape(2, experts * SUB, width)

    def in_order(mine, other):
        return jnp.where(core == 0, mine, other), jnp.where(core == 0, other, mine)

    ids_t = expert_ids.T
    probs_t = gate_probs.T
    rows = exchange(dispatch(ids_t, probs_t, patches, experts, False))
    sent_grads = dispatch(ids_t, probs_t, out_grad, experts, True)
    grads = exchange(sent_grads)

    pair_weights = jnp.concatenate(
        in_order(w_gate[0], swap(w_gate[0])) + in_order(w_up[0], swap(w_up[0])), axis=1
    )
    down_weights = jnp.concatenate(in_order(w_down[0], swap(w_down[0])), axis=1)
    pair_weights, down_weights = lax.optimization_barrier((pair_weights, down_weights))

    gate_pre, up_pre, hidden, expert_out = forward(rows, pair_weights, down_weights)
    back_out = exchange(expert_out)
    gate_grad, up_grad, dx_slots = backward(
        grads, gate_pre, up_pre, pair_weights, down_weights
    )
    back_grad = exchange(dx_slots)

    down_grad = down_grads(core_id, hidden, swap(hidden), grads, swap(grads))
    gate_wgrad, up_wgrad = pair_grads(
        core_id,
        rows,
        swap(rows),
        (gate_grad, swap(gate_grad), up_grad, swap(up_grad)),
    )

    mixed, select = mix(expert_ids, gate_probs, back_out.reshape(-1, width))
    patch_grad = add_routes(select, back_grad.reshape(-1, width))
    return mixed, patch_grad, gate_wgrad[None], up_wgrad[None], down_grad[None]


def solution(mesh):
    in_specs = (
        P("expert", "dp"),
        P("expert", None),
        P("expert", None),
        P("expert", "dp"),
        P("expert", None, "dp"),
        P("expert", None, "dp"),
        P("expert", None, "dp"),
    )
    out_specs = (
        P("expert", "dp"),
        P("expert", "dp"),
        P("expert", None, "dp"),
        P("expert", None, "dp"),
        P("expert", None, "dp"),
    )

    return jax.shard_map(body, mesh=mesh, in_specs=in_specs, out_specs=out_specs, check_vma=False)
```

time: 181 us -> 169 us (0.934)
  matrix products: 61.3 us -> 0 us
  Pallas kernels: 0 us -> 55.8 us
  local copies, waits for them, and re-layouts: 8.5 us -> 3.01 us
  starting transfers between devices: 33.8 us -> 36.8 us
  waiting for transfers between devices: 57.4 us -> 54.4 us
    dot_general x19 -> x0, matrix products: 61.3 us -> none  [dot(): lax.dot_general(left, right, ((left_dims, right_dims), ((), ())), preferr...]
    pallas_call x0 -> x8, Pallas kernels: none -> 55.8 us  [the longest x1 15 us: backward(): pl.pallas_call(backward_kernel, grid=(BLOCKS,), in_specs=[pl.BlockSpec((c...]
    concatenate x2, other arithmetic: 4.16 us -> 8.78 us  [the longest x1 4.88 us: body(): down_weights = jnp.concatenate(in_order(w_down[0], swap(w_down[0])), axis=1)]
    unnamed x45 -> x16, local copies, waits for them, and re-layouts: 6.28 us -> 3.01 us
    all_to_all x4, waiting for transfers between devices: 57.4 us -> 54.3 us  [exchange(): lax.all_to_all(value.reshape(2 * experts, SUB, width), ('dp', 'expert'),...]
    another operation x2 -> x0, other arithmetic: 3 us -> none  [the longest x1 1.5 us: body(): jnp.stack([dot(hidden, down_weights[i], (1,), (0,)).astype(BF16) for i in...]
    squeeze x1 -> x0, local copies, waits for them, and re-layouts: 1.86 us -> none  [body(): rows_full = jnp.concatenate([rows[0], rows[1]], axis=1)]
    select_n x5 -> x3, other arithmetic: 10.2 us -> 8.38 us  [in_order(): jnp.where(core == 0, mine, other)]
  transfers between devices with their start and end apart: 12 -> 12, of which waited for: 4 -> 4; matrix products, arithmetic and copies ran while one was open for 32% -> 11% of each run, Pallas kernels for 0% -> 28%
where the time goes in v2:
time: 169 us; the launch traced here: 168 us
  Pallas kernels  55.8 us (33%)
  waiting for transfers between devices  54.4 us (32%)
  starting transfers between devices  36.8 us (22%)
  other arithmetic  17.2 us (10%)
  local copies, waits for them, and re-layouts  3.01 us (2%)
    all_to_all x4, waiting for transfers between devices, exchange(): lax.all_to_all(value.reshape(2 * experts, SUB, width), ('dp', 'expert'),...  54.3 us
    all_to_all x4, starting transfers between devices, exchange(): lax.all_to_all(value.reshape(2 * experts, SUB, width), ('dp', 'expert'),...  30.9 us
    pallas_call x1, Pallas kernels, backward(): pl.pallas_call(backward_kernel, grid=(BLOCKS,), in_specs=[pl.BlockSpec((c...  15 us
    pallas_call x1, Pallas kernels, forward(): pl.pallas_call(forward_kernel, grid=(BLOCKS,), in_specs=[pl.BlockSpec(mem...  13.8 us
    pallas_call x2, Pallas kernels, share_call(): pl.pallas_call(kernel, out_shape=[shape] * outs, grid_spec=grid_spec)  13.4 us
    select_n x3, other arithmetic, in_order(): jnp.where(core == 0, mine, other)  8.38 us
    pallas_call x2, Pallas kernels, dispatch(): pl.pallas_call(functools.partial(dispatch_kernel, weighted, experts), out...  6.61 us
    ppermute x8, starting transfers between devices, swap(): return lax.ppermute(value, 'dp', [(0, 1), (1, 0)])  5.93 us
  transfers between devices with their start and end apart: 12, of which 4 were waited for; matrix products, arithmetic and copies ran while one was open for 11% of the time, Pallas kernels for 28%

profile of v2, /device:TPU:1, one launch (start us, length us, event | category | flops | bytes accessed | tf_op | source)
XLA Modules:
  0.0 167.9 jit_solution(2193337171416350852)
XLA Ops:
  0.6 1.5 collective-permute-start.2
  2.1 3.2 %send_rows.1 = bf16[1024,1024]{1,0:T(8,128)(2,1)} custom-call(s32[2,160]{1,0:T(2,128)} %bitcast.37, f32[2,160]{1,0:T(2,128)} %bitcast.39, bf16[160,1024]{1,0:T(8,128)(2,1)} %x_ref.2), custom_call_target="tpu_custom_call" | custom-call | tf_op jit(solution)/shard_map/send_rows/pallas_call | solution.py:68
  5.3 10.2 %all-to-all-start = ((bf16[128,8,1024]{2,1,0:T(8,128)(2,1)}), bf16[128,8,1024]{2,1,0:T(8,128)(2,1)S(1)}, u32[]{:S(2)}, u32[]{:S(2)}) async-start(bf16[128,8,1024]{2,1,0:T(8,128)(2,1)} %bitcast.30), calls=%async_computation | async-start | bytes 4194304 | tf_op jit(solution)/shard_map/all_to_all | solution.py:337
  15.5 1.1 collective-permute-start.1
  16.7 0.1 collective-permute-start
  16.8 3.4 %send_grads.1 = bf16[1024,1024]{1,0:T(8,128)(2,1)} custom-call(s32[2,160]{1,0:T(2,128)} %bitcast.38, f32[2,160]{1,0:T(2,128)} %bitcast.40, bf16[160,1024]{1,0:T(8,128)(2,1)} %x_ref.3), custom_call_target="tpu_custom_call" | custom-call | tf_op jit(solution)/shard_map/send_grads/pallas_call | solution.py:68
  20.2 4.5 %broadcast_select_fusion.1 = (bf16[1024,1024]{1,0:T(8,128)(2,1)}, bf16[1024,1024]{1,0:T(8,128)(2,1)}) fusion(bf16[1024,1024]{1,0:T(8,128)(2,1)} %collective-permute-done.2, pred[]{:T(512)S(6)} %eq.2, bf16[1,1024,1024]{2,1,0:T(8,128)(2,1)} %param.13), kind=kLoop, calls=%fused_computation.3 | loop fusion | flops 2097152 | bytes 8388609 | tf_op jit(solution)/shard_map/jit(_where)/select_n | solution.py:346
  24.7 19.5 %all-to-all-done = bf16[128,8,1024]{2,1,0:T(8,128)(2,1)S(1)} async-done(((bf16[128,8,1024]{2,1,0:T(8,128)(2,1)}), bf16[128,8,1024]{2,1,0:T(8,128)(2,1)S(1)}, u32[]{:S(2)}, u32[]{:S(2)}) %all-to-all-start) | async-done | bytes 2097184 | tf_op jit(solution)/shard_map/all_to_all | solution.py:337
  44.2 1.3 copy-done.1
  45.5 6.0 %all-to-all-start.2 = ((bf16[128,8,1024]{2,1,0:T(8,128)(2,1)}), bf16[128,8,1024]{2,1,0:T(8,128)(2,1)S(1)}, u32[]{:S(2)}, u32[]{:S(2)}) async-start(bf16[128,8,1024]{2,1,0:T(8,128)(2,1)} %bitcast.29), calls=%async_computation.2 | async-start | bytes 4194304 | tf_op jit(solution)/shard_map/all_to_all | solution.py:337
  51.5 4.9 %pad_maximum_fusion.1.wd_hbm.wd_ref = bf16[1024,2048]{1,0:T(8,128)(2,1)} fusion(bf16[1024,1024]{1,0:T(8,128)(2,1)} %get-tuple-element.32, bf16[1024,1024]{1,0:T(8,128)(2,1)} %get-tuple-element.31), kind=kLoop, calls=%fused_computation.1 | loop fusion | flops 8388608 | bytes 8388608 | tf_op jit(solution)/shard_map/concatenate | solution.py:357
  56.4 2.0 %broadcast_select_fusion.3 = (bf16[2048,512]{1,0:T(8,128)(2,1)S(1)}, bf16[2048,512]{1,0:T(8,128)(2,1)S(1)}) fusion(bf16[2048,512]{1,0:T(8,128)(2,1)} %collective-permute-done.1, pred[]{:T(512)S(6)} %eq.2, bf16[1,2048,512]{2,1,0:T(8,128)(2,1)S(1)} %copy-done.2), kind=kLoop, calls=%fused_computation.5 | loop fusion | flops 2097152 | bytes 8388609 | tf_op jit(solution)/shard_map/jit(_where)/select_n | solution.py:346
  58.4 0.2 copy-done.3
  58.6 1.9 %broadcast_select_fusion.5 = (bf16[2048,512]{1,0:T(8,128)(2,1)S(1)}, bf16[2048,512]{1,0:T(8,128)(2,1)S(1)}) fusion(bf16[2048,512]{1,0:T(8,128)(2,1)} %collective-permute-done, pred[]{:T(512)S(6)} %eq.2, bf16[1,2048,512]{2,1,0:T(8,128)(2,1)S(1)} %copy-done.3), kind=kLoop, calls=%fused_computation.7 | loop fusion | flops 2097152 | bytes 8388609 | tf_op jit(solution)/shard_map/jit(_where)/select_n | solution.py:346
  60.5 3.9 %pad_maximum_fusion.wg_ref.wu_ref.wp_hbm = bf16[2048,2048]{1,0:T(8,128)(2,1)} fusion(bf16[2048,512]{1,0:T(8,128)(2,1)S(1)} %get-tuple-element.36, bf16[2048,512]{1,0:T(8,128)(2,1)S(1)} %get-tuple-element.35, bf16[2048,512]{1,0:T(8,128)(2,1)S(1)} %get-tuple-element.34, bf16[2048,512]{1,0:T(8,128)(2,1)S(1)} %get-tuple-element.33), kind=kLoop, calls=%fused_computation | loop fusion | flops 33554432 | bytes 16777216 | tf_op jit(solution)/shard_map/concatenate | solution.py:354
  64.4 13.8 %forward.1 = (f32[512,1024]{1,0:T(8,128)}, f32[512,1024]{1,0:T(8,128)}, bf16[512,1024]{1,0:T(8,128)(2,1)}, bf16[2,512,1024]{2,1,0:T(8,128)(2,1)}) custom-call(bf16[2,512,1024]{2,1,0:T(8,128)(2,1)} %bitcast.26, bf16[2048,2048]{1,0:T(8,128)(2,1)} %pad_maximum_fusion.wg_ref.wu_ref.wp_hbm, bf16[2048,2048]{1,0:T(8,128)(2,1)} %pad_maximum_fusion.wg_ref.wu_ref.wp_hbm, ...), custom_call_target="tpu_custom_call" | custom-call | tf_op jit(solution)/shard_map/forward/pallas_call | solution.py:181
  78.1 2.0 %all-to-all-done.2 = bf16[128,8,1024]{2,1,0:T(8,128)(2,1)S(1)} async-done(((bf16[128,8,1024]{2,1,0:T(8,128)(2,1)}), bf16[128,8,1024]{2,1,0:T(8,128)(2,1)S(1)}, u32[]{:S(2)}, u32[]{:S(2)}) %all-to-all-start.2) | async-done | bytes 2097184 | tf_op jit(solution)/shard_map/all_to_all | solution.py:337
  80.2 8.2 %all-to-all-start.1 = ((bf16[128,8,1024]{2,1,0:T(8,128)(2,1)}), bf16[128,8,1024]{2,1,0:T(8,128)(2,1)}, u32[]{:S(2)}, u32[]{:S(2)}) async-start(bf16[128,8,1024]{2,1,0:T(8,128)(2,1)} %bitcast.32), calls=%async_computation.1 | async-start | bytes 4194304 | tf_op jit(solution)/shard_map/all_to_all | solution.py:337
  88.4 1.2 collective-permute-start.7
  89.6 0.3 collective-permute-start.3
  89.9 15.0 %backward.1 = (bf16[512,1024]{1,0:T(8,128)(2,1)}, bf16[512,1024]{1,0:T(8,128)(2,1)}, bf16[2,512,1024]{2,1,0:T(8,128)(2,1)}) custom-call(bf16[2,512,1024]{2,1,0:T(8,128)(2,1)} %bitcast.24, f32[512,1024]{1,0:T(8,128)} %get-tuple-element.23.gp_ref, f32[512,1024]{1,0:T(8,128)} %get-tuple-element.24.up_ref, bf16[1024,2048]{1,0:T(8,128)(2,1)} %pad_maximum_fusion.1.wd_hbm.wd_ref, ...), custom_call_target="tpu_custom_call" | custom-call | tf_op jit(solution)/shard_map/backward/pallas_call | solution.py:252
  104.9 11.8 %all-to-all-done.1 = bf16[128,8,1024]{2,1,0:T(8,128)(2,1)} async-done(((bf16[128,8,1024]{2,1,0:T(8,128)(2,1)}), bf16[128,8,1024]{2,1,0:T(8,128)(2,1)}, u32[]{:S(2)}, u32[]{:S(2)}) %all-to-all-start.1) | async-done | bytes 2097184 | tf_op jit(solution)/shard_map/all_to_all | solution.py:337
  116.7 6.5 %all-to-all-start.3 = ((bf16[128,8,1024]{2,1,0:T(8,128)(2,1)}), bf16[128,8,1024]{2,1,0:T(8,128)(2,1)}, u32[]{:S(2)}, u32[]{:S(2)}) async-start(bf16[128,8,1024]{2,1,0:T(8,128)(2,1)} %bitcast.31), calls=%async_computation.3 | async-start | bytes 4194304 | tf_op jit(solution)/shard_map/all_to_all | solution.py:337
  123.2 1.2 collective-permute-start.6
  124.5 0.4 collective-permute-start.5
  124.9 0.8 copy.12.ids_ref
  125.7 0.8 copy.13.probs_ref
  126.4 4.0 %mix.1 = (bf16[160,1024]{1,0:T(8,128)(2,1)}, bf16[160,1024]{1,0:T(8,128)(2,1)}) custom-call(s32[160,2]{1,0:T(8,128)} %copy.12.ids_ref, f32[160,2]{1,0:T(8,128)} %copy.13.probs_ref, bf16[1024,1024]{1,0:T(8,128)(2,1)} %bitcast.8.back_hbm), custom_call_target="tpu_custom_call" | custom-call | tf_op jit(solution)/shard_map/mix/pallas_call | solution.py:101
  130.4 21.0 %all-to-all-done.3 = bf16[128,8,1024]{2,1,0:T(8,128)(2,1)} async-done(((bf16[128,8,1024]{2,1,0:T(8,128)(2,1)}), bf16[128,8,1024]{2,1,0:T(8,128)(2,1)}, u32[]{:S(2)}, u32[]{:S(2)}) %all-to-all-start.3) | async-done | bytes 2097184 | tf_op jit(solution)/shard_map/all_to_all | solution.py:337
  151.5 3.0 %add_routes.1 = bf16[160,1024]{1,0:T(8,128)(2,1)} custom-call(bf16[160,1024]{1,0:T(8,128)(2,1)} %get-tuple-element.22.select_ref, bf16[1024,1024]{1,0:T(8,128)(2,1)} %bitcast.12.back_ref), custom_call_target="tpu_custom_call" | custom-call | tf_op jit(solution)/shard_map/add_routes/pallas_call | solution.py:118
  154.4 5.4 %shard_map.111 = bf16[1024,1024]{1,0:T(8,128)(2,1)} custom-call(s32[1]{0:T(128)} %bitcast.13.core_ref, bf16[512,1024]{1,0:T(8,128)(2,1)} %get-tuple-element.30.h_ref, bf16[512,1024]{1,0:T(8,128)(2,1)} %collective-permute-done.6.hp_ref, bf16[2,512,1024]{2,1,0:T(8,128)(2,1)} %bitcast.25, bf16[2,512,1024]{2,1,0:T(8,128)(2,1)} %collective-permute-done.7.gp_ref), custom_call_target="tpu_custom_call" | custom-call | tf_op jit(solution)/shard_map/pallas_call | solution.py:301
  159.9 8.0 %shard_map.110 = (bf16[2048,512]{1,0:T(8,128)(2,1)}, bf16[2048,512]{1,0:T(8,128)(2,1)}) custom-call(s32[1]{0:T(128)} %bitcast.13.core_ref, bf16[2,512,1024]{2,1,0:T(8,128)(2,1)} %bitcast.28, bf16[2,512,1024]{2,1,0:T(8,128)(2,1)} %collective-permute-done.3.xp_ref, bf16[512,1024]{1,0:T(8,128)(2,1)} %get-tuple-element.26.g_ref, ...), custom_call_target="tpu_custom_call" | custom-call | tf_op jit(solution)/shard_map/pallas_call | solution.py:301
  (21 shorter events, 0.1 us)
Async XLA Ops:
  0.6 19.5 %collective-permute-start.2 = (bf16[1024,1024]{1,0:T(8,128)(2,1)}, bf16[1024,1024]{1,0:T(8,128)(2,1)}, u32[]{:S(2)}, u32[]{:S(2)}) collective-permute-start(bf16[1024,1024]{1,0:T(8,128)(2,1)} %bitcast.33), channel_id=1, source_target_pairs={{0,64},{64,0},{1,65},{65,1},{2,66},{66,2},{3,67},{67,3},{4,68},{68... | collective-permute-start | bytes 6291464 | tf_op jit(solution)/shard_map/ppermute | solution.py:334
  5.3 38.9 %all-to-all-start = ((bf16[128,8,1024]{2,1,0:T(8,128)(2,1)}), bf16[128,8,1024]{2,1,0:T(8,128)(2,1)S(1)}, u32[]{:S(2)}, u32[]{:S(2)}) async-start(bf16[128,8,1024]{2,1,0:T(8,128)(2,1)} %bitcast.30), calls=%async_computation | async-start | bytes 4194304 | tf_op jit(solution)/shard_map/all_to_all | solution.py:337
  15.5 40.9 %collective-permute-start.1 = (bf16[2048,512]{1,0:T(8,128)(2,1)}, bf16[2048,512]{1,0:T(8,128)(2,1)}, u32[]{:S(2)}, u32[]{:S(2)}) collective-permute-start(bf16[2048,512]{1,0:T(8,128)(2,1)} %bitcast.34), channel_id=1, source_target_pairs={{0,64},{64,0},{1,65},{65,1},{2,66},{66,2},{3,67},{67,3},{4,68},{68... | collective-permute-start | bytes 6291464 | tf_op jit(solution)/shard_map/ppermute | solution.py:334
  16.7 41.7 %collective-permute-start = (bf16[2048,512]{1,0:T(8,128)(2,1)}, bf16[2048,512]{1,0:T(8,128)(2,1)}, u32[]{:S(2)}, u32[]{:S(2)}) collective-permute-start(bf16[2048,512]{1,0:T(8,128)(2,1)} %bitcast.35), channel_id=1, source_target_pairs={{0,64},{64,0},{1,65},{65,1},{2,66},{66,2},{3,67},{67,3},{4,68},{68... | collective-permute-start | bytes 6291464 | tf_op jit(solution)/shard_map/ppermute | solution.py:334
  44.2 1.3 copy-start.1
  45.5 34.7 %all-to-all-start.2 = ((bf16[128,8,1024]{2,1,0:T(8,128)(2,1)}), bf16[128,8,1024]{2,1,0:T(8,128)(2,1)S(1)}, u32[]{:S(2)}, u32[]{:S(2)}) async-start(bf16[128,8,1024]{2,1,0:T(8,128)(2,1)} %bitcast.29), calls=%async_computation.2 | async-start | bytes 4194304 | tf_op jit(solution)/shard_map/all_to_all | solution.py:337
  51.5 4.9 %copy-start.2 = (bf16[1,2048,512]{2,1,0:T(8,128)(2,1)S(1)}, bf16[1,2048,512]{2,1,0:T(8,128)(2,1)}, u32[]{:S(2)}) copy-start(bf16[1,2048,512]{2,1,0:T(8,128)(2,1)} %param.12) | copy-start | bytes 6291460
  56.4 2.2 %copy-start.3 = (bf16[1,2048,512]{2,1,0:T(8,128)(2,1)S(1)}, bf16[1,2048,512]{2,1,0:T(8,128)(2,1)}, u32[]{:S(2)}) copy-start(bf16[1,2048,512]{2,1,0:T(8,128)(2,1)} %param.11) | copy-start | bytes 6291460
  80.2 8.2 %copy-start = (bf16[128,8,1024]{2,1,0:T(8,128)(2,1)}, bf16[128,8,1024]{2,1,0:T(8,128)(2,1)S(1)}, u32[]{:S(2)}) copy-start(bf16[128,8,1024]{2,1,0:T(8,128)(2,1)S(1)} %all-to-all-done.2) | copy-start | bytes 6291460
  80.2 36.5 %all-to-all-start.1 = ((bf16[128,8,1024]{2,1,0:T(8,128)(2,1)}), bf16[128,8,1024]{2,1,0:T(8,128)(2,1)}, u32[]{:S(2)}, u32[]{:S(2)}) async-start(bf16[128,8,1024]{2,1,0:T(8,128)(2,1)} %bitcast.32), calls=%async_computation.1 | async-start | bytes 4194304 | tf_op jit(solution)/shard_map/all_to_all | solution.py:337
  88.4 66.1 %collective-permute-start.7 = (bf16[2,512,1024]{2,1,0:T(8,128)(2,1)S(1)}, bf16[2,512,1024]{2,1,0:T(8,128)(2,1)}, u32[]{:S(2)}, u32[]{:S(2)}) collective-permute-start(bf16[2,512,1024]{2,1,0:T(8,128)(2,1)S(1)} %bitcast.23), channel_id=1, source_target_pairs={{0,64},{64,0},{1,65},{65,1},{2,66},{66,2},{3,67},{67,3},{4,68},{68... | collective-permute-start | bytes 6291464 | tf_op jit(solution)/shard_map/ppermute | solution.py:334
  89.6 70.3 %collective-permute-start.3 = (bf16[2,512,1024]{2,1,0:T(8,128)(2,1)}, bf16[2,512,1024]{2,1,0:T(8,128)(2,1)}, u32[]{:S(2)}, u32[]{:S(2)}) collective-permute-start(bf16[2,512,1024]{2,1,0:T(8,128)(2,1)} %bitcast.27), channel_id=1, source_target_pairs={{0,64},{64,0},{1,65},{65,1},{2,66},{66,2},{3,67},{67,3},{4,68},{68... | collective-permute-start | bytes 6291464 | tf_op jit(solution)/shard_map/ppermute | solution.py:334
  116.7 6.5 %copy-start.4 = (bf16[512,1024]{1,0:T(8,128)(2,1)S(1)}, bf16[512,1024]{1,0:T(8,128)(2,1)}, u32[]{:S(2)}) copy-start(bf16[512,1024]{1,0:T(8,128)(2,1)} %get-tuple-element.30.h_ref) | copy-start | bytes 3145732
  116.7 8.2 %copy-start.5 = (s32[160,2]{0,1:T(2,128)S(1)}, s32[160,2]{0,1:T(2,128)}, u32[]{:S(2)}) copy-start(s32[160,2]{0,1:T(2,128)} %param.8) | copy-start | bytes 3844
  116.7 9.0 %copy-start.6 = (f32[160,2]{0,1:T(2,128)S(1)}, f32[160,2]{0,1:T(2,128)}, u32[]{:S(2)}) copy-start(f32[160,2]{0,1:T(2,128)} %param.9) | copy-start | bytes 3844
  116.7 34.8 %all-to-all-start.3 = ((bf16[128,8,1024]{2,1,0:T(8,128)(2,1)}), bf16[128,8,1024]{2,1,0:T(8,128)(2,1)}, u32[]{:S(2)}, u32[]{:S(2)}) async-start(bf16[128,8,1024]{2,1,0:T(8,128)(2,1)} %bitcast.31), calls=%async_computation.3 | async-start | bytes 4194304 | tf_op jit(solution)/shard_map/all_to_all | solution.py:337
  123.2 31.3 %collective-permute-start.6 = (bf16[512,1024]{1,0:T(8,128)(2,1)S(1)}, bf16[512,1024]{1,0:T(8,128)(2,1)}, u32[]{:S(2)}, u32[]{:S(2)}) collective-permute-start(bf16[512,1024]{1,0:T(8,128)(2,1)S(1)} %copy-done.4), channel_id=1, source_target_pairs={{0,64},{64,0},{1,65},{65,1},{2,66},{66,2},{3,67},{67,3},{4,68},{68... | collective-permute-start | bytes 3145736 | tf_op jit(solution)/shard_map/ppermute | solution.py:334
  124.4 35.5 %collective-permute-start.4 = (bf16[512,1024]{1,0:T(8,128)(2,1)}, bf16[512,1024]{1,0:T(8,128)(2,1)}, u32[]{:S(2)}, u32[]{:S(2)}) collective-permute-start(bf16[512,1024]{1,0:T(8,128)(2,1)} %get-tuple-element.26.g_ref), channel_id=1, source_target_pairs={{0,64},{64,0},{1,65},{65,1},{2,66},{66,2},{3,67},{67,3},{4,68},{68... | collective-permute-start | bytes 3145736 | tf_op jit(solution)/shard_map/ppermute | solution.py:334
  124.5 35.4 %collective-permute-start.5 = (bf16[512,1024]{1,0:T(8,128)(2,1)}, bf16[512,1024]{1,0:T(8,128)(2,1)}, u32[]{:S(2)}, u32[]{:S(2)}) collective-permute-start(bf16[512,1024]{1,0:T(8,128)(2,1)} %get-tuple-element.27.u_ref), channel_id=1, source_target_pairs={{0,64},{64,0},{1,65},{65,1},{2,66},{66,2},{3,67},{67,3},{4,68},{68... | collective-permute-start | bytes 3145736 | tf_op jit(solution)/shard_map/ppermute | solution.py:334

commit v3 on v2

--- a/solution.py
+++ b/solution.py
@@ -15,6 +15,7 @@
 BLOCKS = 4
 HBM = pl.BlockSpec(memory_space=pl.ANY)
 VMEM = pl.BlockSpec(memory_space=pltpu.VMEM)
+GRANT = 64000 * 1024
 
 
 def dot(left, right, left_dims, right_dims):
@@ -48,30 +49,45 @@
     return slots
 
 
-def dispatch_kernel(weighted, experts, ids_ref, probs_ref, x_ref, out_ref):
+def dispatch_kernel(experts, ids_ref, x_ref, *refs):
+    weighted = len(refs) == 4
+    out_hbm, out_ref, sems = refs[-3:]
     tok = x_ref.shape[0]
-    chunk = out_ref.shape[0] // BLOCKS
+    rows = out_ref.shape[0]
+    start = 0
     slots = slots_of([ids_ref[k : k + 1, :] for k in range(2)], 0, experts)
-    for n in range(BLOCKS):
-        spot = lax.broadcasted_iota(I32, (chunk, tok), 0) + n * chunk
+    saves = []
+    for n, chunk in enumerate((rows // 2, rows // 4, rows // 8, rows // 8)):
+        here = pl.ds(start, chunk)
+        spot = lax.broadcasted_iota(I32, (chunk, tok), 0) + start
         hits = [spot == slots[k] for k in range(2)]
         value = mm(one_hot(hits[0] | hits[1]), x_ref[...])
         if weighted:
+            probs_ref = refs[0]
             probs = jnp.where(hits[0], probs_ref[0:1, :], 0.0) + jnp.where(
                 hits[1], probs_ref[1:2, :], 0.0
             )
             value = value * jnp.sum(probs, axis=1, keepdims=True)
-        out_ref[n * chunk : (n + 1) * chunk, :] = value.astype(BF16)
-
-
-def dispatch(ids_t, probs_t, source, experts, weighted):
+        out_ref[start : start + chunk, :] = value.astype(BF16)
+        saves.append(pltpu.make_async_copy(out_ref.at[here], out_hbm.at[here], sems.at[n]))
+        saves[n].start()
+        start += chunk
+    for save in saves:
+        save.wait()
+
+
+def dispatch(experts, ids_t, source, *probs_t):
+    rows, width = 2 * experts * SUB, source.shape[1]
+    weighted = len(probs_t) == 1
     return pl.pallas_call(
-        functools.partial(dispatch_kernel, weighted, experts),
-        out_shape=jax.ShapeDtypeStruct((2 * experts * SUB, source.shape[1]), BF16),
-        in_specs=[VMEM] * 3,
-        out_specs=VMEM,
+        functools.partial(dispatch_kernel, experts),
+        out_shape=jax.ShapeDtypeStruct((rows, width), BF16),
+        in_specs=[VMEM] * (2 + len(probs_t)),
+        out_specs=HBM,
+        scratch_shapes=[pltpu.VMEM((rows, width), BF16), pltpu.SemaphoreType.DMA((BLOCKS,))],
+        compiler_params=pltpu.CompilerParams(vmem_limit_bytes=GRANT) if weighted else None,
         name="send_grads" if weighted else "send_rows",
-    )(ids_t, probs_t, source)
+    )(ids_t, source, *probs_t)
 
 
 def mix_kernel(ids_ref, probs_ref, back_hbm, out_ref, select_ref, back_ref, sems):
@@ -110,20 +126,6 @@
     )(ids, probs, back)
 
 
-def add_kernel(select_ref, back_ref, out_ref):
-    out_ref[...] = mm(select_ref[...], back_ref[...]).astype(BF16)
-
-
-def add_routes(select, back):
-    return pl.pallas_call(
-        add_kernel,
-        out_shape=jax.ShapeDtypeStruct((select.shape[0], back.shape[1]), BF16),
-        in_specs=[VMEM, VMEM],
-        out_specs=VMEM,
-        name="add_routes",
-    )(select, back)
-
-
 def write_halves(value_of, stage_ref, out_hbm, sems):
     copies = []
     for half in range(2):
@@ -347,8 +349,8 @@
 
     ids_t = expert_ids.T
     probs_t = gate_probs.T
-    rows = exchange(dispatch(ids_t, probs_t, patches, experts, False))
-    sent_grads = dispatch(ids_t, probs_t, out_grad, experts, True)
+    rows = exchange(dispatch(experts, ids_t, patches))
+    sent_grads = dispatch(experts, ids_t, out_grad, probs_t)
     grads = exchange(sent_grads)
 
     pair_weights = jnp.concatenate(
@@ -373,7 +375,7 @@
     )
 
     mixed, select = mix(expert_ids, gate_probs, back_out.reshape(-1, width))
-    patch_grad = add_routes(select, back_grad.reshape(-1, width))
+    patch_grad = mm(select, back_grad.reshape(-1, width)).astype(BF16)
     return mixed, patch_grad, gate_wgrad[None], up_wgrad[None], down_grad[None]
 
 

time: 169 us -> 162 us (0.959)
  waiting for transfers between devices: 54.4 us -> 48 us
  Pallas kernels: 55.8 us -> 52.2 us
  matrix products: 0 us -> 2.83 us
    all_to_all x4, waiting for transfers between devices: 54.3 us -> 48 us  [exchange(): lax.all_to_all(value.reshape(2 * experts, SUB, width), ('dp', 'expert'),...]
    pallas_call x3 -> x2, Pallas kernels: 9.56 us -> 6.06 us  [dispatch(): pl.pallas_call(functools.partial(dispatch_kernel, experts), out_shape=jax...]
    dot_general x0 -> x1, matrix products: none -> 2.83 us  [dot(): lax.dot_general(left, right, ((left_dims, right_dims), ((), ())), preferr...]
  transfers between devices with their start and end apart: 12 -> 12, of which waited for: 4 -> 4; matrix products, arithmetic and copies ran while one was open for 11% -> 14% of each run, Pallas kernels for 28% -> 27%
where the time goes in v3:
time: 162 us
  Pallas kernels  52.2 us (32%)
  waiting for transfers between devices  48 us (30%)
  starting transfers between devices  38.1 us (24%)
  other arithmetic  18.1 us (11%)
  matrix products  2.83 us (2%)
    all_to_all x4, waiting for transfers between devices, exchange(): lax.all_to_all(value.reshape(2 * experts, SUB, width), ('dp', 'expert'),...  48 us
    all_to_all x4, starting transfers between devices, exchange(): lax.all_to_all(value.reshape(2 * experts, SUB, width), ('dp', 'expert'),...  32.1 us
    pallas_call x1, Pallas kernels, backward(): pl.pallas_call(backward_kernel, grid=(BLOCKS,), in_specs=[pl.BlockSpec((c...  14.9 us
    pallas_call x1, Pallas kernels, forward(): pl.pallas_call(forward_kernel, grid=(BLOCKS,), in_specs=[pl.BlockSpec(mem...  13.8 us
    pallas_call x2, Pallas kernels, share_call(): pl.pallas_call(kernel, out_shape=[shape] * outs, grid_spec=grid_spec)  13.5 us
    select_n x3, other arithmetic, in_order(): jnp.where(core == 0, mine, other)  9.5 us
    pallas_call x2, Pallas kernels, dispatch(): pl.pallas_call(functools.partial(dispatch_kernel, experts), out_shape=jax...  6.06 us
    ppermute x8, starting transfers between devices, swap(): return lax.ppermute(value, 'dp', [(0, 1), (1, 0)])  6 us
  transfers between devices with their start and end apart: 12, of which 4 were waited for; matrix products, arithmetic and copies ran while one was open for 14% of the time, Pallas kernels for 27%

profile of v3, /device:TPU:1, one launch (start us, length us, event | category | flops | bytes accessed | tf_op | source)
XLA Modules:
  0.0 161.6 jit_solution(6029261459695767650)
XLA Ops:
  0.6 1.5 collective-permute-start.2
  2.1 2.9 %send_rows.1 = bf16[1024,1024]{1,0:T(8,128)(2,1)} custom-call(s32[2,160]{1,0:T(2,128)} %bitcast.37, bf16[160,1024]{1,0:T(8,128)(2,1)} %x_ref.2), custom_call_target="tpu_custom_call" | custom-call | tf_op jit(solution)/shard_map/send_rows/pallas_call | solution.py:82
  5.0 10.7 %all-to-all-start = ((bf16[128,8,1024]{2,1,0:T(8,128)(2,1)}), bf16[128,8,1024]{2,1,0:T(8,128)(2,1)}, u32[]{:S(2)}, u32[]{:S(2)}) async-start(bf16[128,8,1024]{2,1,0:T(8,128)(2,1)} %bitcast.32), calls=%async_computation | async-start | bytes 4194304 | tf_op jit(solution)/shard_map/all_to_all | solution.py:339
  15.7 1.2 collective-permute-start.1
  16.9 0.1 collective-permute-start
  17.0 3.1 %send_grads.1 = bf16[1024,1024]{1,0:T(8,128)(2,1)} custom-call(s32[2,160]{1,0:T(2,128)} %bitcast.38, bf16[160,1024]{1,0:T(8,128)(2,1)} %x_ref.3, f32[2,160]{1,0:T(2,128)} %bitcast.39), custom_call_target="tpu_custom_call" | custom-call | tf_op jit(solution)/shard_map/send_grads/pallas_call | solution.py:82
  20.2 4.5 %broadcast_select_fusion.1 = (bf16[1024,1024]{1,0:T(8,128)(2,1)}, bf16[1024,1024]{1,0:T(8,128)(2,1)}) fusion(bf16[1024,1024]{1,0:T(8,128)(2,1)} %collective-permute-done.2, pred[]{:T(512)S(6)} %eq.2, bf16[1,1024,1024]{2,1,0:T(8,128)(2,1)} %param.13), kind=kLoop, calls=%fused_computation.5 | loop fusion | flops 2097152 | bytes 8388609 | tf_op jit(solution)/shard_map/jit(_where)/select_n | solution.py:348
  24.7 19.3 %all-to-all-done = bf16[128,8,1024]{2,1,0:T(8,128)(2,1)} async-done(((bf16[128,8,1024]{2,1,0:T(8,128)(2,1)}), bf16[128,8,1024]{2,1,0:T(8,128)(2,1)}, u32[]{:S(2)}, u32[]{:S(2)}) %all-to-all-start) | async-done | bytes 2097184 | tf_op jit(solution)/shard_map/all_to_all | solution.py:339
  44.0 6.0 %all-to-all-start.2 = ((bf16[128,8,1024]{2,1,0:T(8,128)(2,1)}), bf16[128,8,1024]{2,1,0:T(8,128)(2,1)S(1)}, u32[]{:S(2)}, u32[]{:S(2)}) async-start(bf16[128,8,1024]{2,1,0:T(8,128)(2,1)} %bitcast.31), calls=%async_computation.2 | async-start | bytes 4194304 | tf_op jit(solution)/shard_map/all_to_all | solution.py:339
  50.0 4.7 %pad_maximum_fusion.1.wd_hbm.wd_ref = bf16[1024,2048]{1,0:T(8,128)(2,1)} fusion(bf16[1024,1024]{1,0:T(8,128)(2,1)} %get-tuple-element.32, bf16[1024,1024]{1,0:T(8,128)(2,1)} %get-tuple-element.31), kind=kLoop, calls=%fused_computation.1 | loop fusion | flops 8388608 | bytes 8388608 | tf_op jit(solution)/shard_map/concatenate | solution.py:359
  54.8 2.5 %broadcast_select_fusion.3 = (bf16[2048,512]{1,0:T(8,128)(2,1)S(1)}, bf16[2048,512]{1,0:T(8,128)(2,1)S(1)}) fusion(bf16[2048,512]{1,0:T(8,128)(2,1)} %collective-permute-done.1, pred[]{:T(512)S(6)} %eq.2, bf16[1,2048,512]{2,1,0:T(8,128)(2,1)} %param.12), kind=kLoop, calls=%fused_computation.7 | loop fusion | flops 2097152 | bytes 8388609 | tf_op jit(solution)/shard_map/jit(_where)/select_n | solution.py:348
  57.3 2.5 %broadcast_select_fusion.5 = (bf16[2048,512]{1,0:T(8,128)(2,1)S(1)}, bf16[2048,512]{1,0:T(8,128)(2,1)S(1)}) fusion(bf16[2048,512]{1,0:T(8,128)(2,1)} %collective-permute-done, pred[]{:T(512)S(6)} %eq.2, bf16[1,2048,512]{2,1,0:T(8,128)(2,1)} %param.11), kind=kLoop, calls=%fused_computation.9 | loop fusion | flops 2097152 | bytes 8388609 | tf_op jit(solution)/shard_map/jit(_where)/select_n | solution.py:348
  59.8 3.9 %pad_maximum_fusion.wg_ref.wu_ref.wp_hbm = bf16[2048,2048]{1,0:T(8,128)(2,1)} fusion(bf16[2048,512]{1,0:T(8,128)(2,1)S(1)} %get-tuple-element.36, bf16[2048,512]{1,0:T(8,128)(2,1)S(1)} %get-tuple-element.35, bf16[2048,512]{1,0:T(8,128)(2,1)S(1)} %get-tuple-element.34, bf16[2048,512]{1,0:T(8,128)(2,1)S(1)} %get-tuple-element.33), kind=kLoop, calls=%fused_computation | loop fusion | flops 33554432 | bytes 16777216 | tf_op jit(solution)/shard_map/concatenate | solution.py:356
  63.7 13.8 %forward.1 = (f32[512,1024]{1,0:T(8,128)}, f32[512,1024]{1,0:T(8,128)}, bf16[512,1024]{1,0:T(8,128)(2,1)}, bf16[2,512,1024]{2,1,0:T(8,128)(2,1)}) custom-call(bf16[2,512,1024]{2,1,0:T(8,128)(2,1)} %bitcast.2.x_hbm.x_ref, bf16[2048,2048]{1,0:T(8,128)(2,1)} %pad_maximum_fusion.wg_ref.wu_ref.wp_hbm, bf16[2048,2048]{1,0:T(8,128)(2,1)} %pad_maximum_fusion.wg_ref.wu_ref.wp_hbm, ...), custom_call_target="tpu_custom_call" | custom-call | tf_op jit(solution)/shard_map/forward/pallas_call | solution.py:183
  77.4 1.3 all-to-all-done.2
  78.7 9.0 %all-to-all-start.1 = ((bf16[128,8,1024]{2,1,0:T(8,128)(2,1)}), bf16[128,8,1024]{2,1,0:T(8,128)(2,1)}, u32[]{:S(2)}, u32[]{:S(2)}) async-start(bf16[128,8,1024]{2,1,0:T(8,128)(2,1)} %bitcast.34), calls=%async_computation.1 | async-start | bytes 4194304 | tf_op jit(solution)/shard_map/all_to_all | solution.py:339
  87.7 1.4 collective-permute-start.7
  89.1 14.9 %backward.1 = (bf16[512,1024]{1,0:T(8,128)(2,1)}, bf16[512,1024]{1,0:T(8,128)(2,1)}, bf16[2,512,1024]{2,1,0:T(8,128)(2,1)}) custom-call(bf16[2,512,1024]{2,1,0:T(8,128)(2,1)} %bitcast.29, f32[512,1024]{1,0:T(8,128)} %get-tuple-element.23.gp_ref, f32[512,1024]{1,0:T(8,128)} %get-tuple-element.24.up_ref, bf16[1024,2048]{1,0:T(8,128)(2,1)} %pad_maximum_fusion.1.wd_hbm.wd_ref, ...), custom_call_target="tpu_custom_call" | custom-call | tf_op jit(solution)/shard_map/backward/pallas_call | solution.py:254
  104.0 12.0 %all-to-all-done.1 = bf16[128,8,1024]{2,1,0:T(8,128)(2,1)} async-done(((bf16[128,8,1024]{2,1,0:T(8,128)(2,1)}), bf16[128,8,1024]{2,1,0:T(8,128)(2,1)}, u32[]{:S(2)}, u32[]{:S(2)}) %all-to-all-start.1) | async-done | bytes 2097184 | tf_op jit(solution)/shard_map/all_to_all | solution.py:339
  116.0 6.5 %all-to-all-start.3 = ((bf16[128,8,1024]{2,1,0:T(8,128)(2,1)}), bf16[128,8,1024]{2,1,0:T(8,128)(2,1)}, u32[]{:S(2)}, u32[]{:S(2)}) async-start(bf16[128,8,1024]{2,1,0:T(8,128)(2,1)} %bitcast.33), calls=%async_computation.3 | async-start | bytes 4194304 | tf_op jit(solution)/shard_map/all_to_all | solution.py:339
  122.5 1.2 collective-permute-start.3
  123.7 0.1 collective-permute-start.6
  123.8 0.4 collective-permute-start.4
  124.2 0.1 collective-permute-start.5
  124.3 0.8 copy.12.ids_ref
  125.0 0.8 copy.13.probs_ref
  125.8 4.0 %mix.1 = (bf16[160,1024]{1,0:T(8,128)(2,1)}, bf16[160,1024]{1,0:T(8,128)(2,1)}) custom-call(s32[160,2]{1,0:T(8,128)} %copy.12.ids_ref, f32[160,2]{1,0:T(8,128)} %copy.13.probs_ref, bf16[1024,1024]{1,0:T(8,128)(2,1)} %bitcast.7.back_hbm), custom_call_target="tpu_custom_call" | custom-call | tf_op jit(solution)/shard_map/mix/pallas_call | solution.py:117
  129.8 0.0 copy-start.2
  129.9 5.5 %shard_map.111 = bf16[1024,1024]{1,0:T(8,128)(2,1)} custom-call(s32[1]{0:T(128)} %bitcast.13.core_ref, bf16[512,1024]{1,0:T(8,128)(2,1)} %get-tuple-element.30.h_ref, bf16[512,1024]{1,0:T(8,128)(2,1)} %collective-permute-done.6.hp_ref, bf16[2,512,1024]{2,1,0:T(8,128)(2,1)} %bitcast.30, bf16[2,512,1024]{2,1,0:T(8,128)(2,1)} %collective-permute-done.7.gp_ref), custom_call_target="tpu_custom_call" | custom-call | tf_op jit(solution)/shard_map/pallas_call | solution.py:303
  135.3 15.4 %all-to-all-done.3 = bf16[128,8,1024]{2,1,0:T(8,128)(2,1)} async-done(((bf16[128,8,1024]{2,1,0:T(8,128)(2,1)}), bf16[128,8,1024]{2,1,0:T(8,128)(2,1)}, u32[]{:S(2)}, u32[]{:S(2)}) %all-to-all-start.3) | async-done | bytes 2097184 | tf_op jit(solution)/shard_map/all_to_all | solution.py:339
  150.8 2.8 %fusion.2 = bf16[160,1024]{1,0:T(8,128)(2,1)} fusion(bf16[160,1024]{1,0:T(8,128)(2,1)S(1)} %copy-done.2, bf16[128,8,1024]{2,1,0:T(8,128)(2,1)} %all-to-all-done.3), kind=kOutput, calls=%fused_computation.10 | convolution fusion | flops 335708160 | bytes 2752512 | tf_op jit(solution)/shard_map/dot_general | solution.py:22
  153.6 8.0 %shard_map.110 = (bf16[2048,512]{1,0:T(8,128)(2,1)}, bf16[2048,512]{1,0:T(8,128)(2,1)}) custom-call(s32[1]{0:T(128)} %bitcast.13.core_ref, bf16[2,512,1024]{2,1,0:T(8,128)(2,1)} %bitcast.2.x_hbm.x_ref, bf16[2,512,1024]{2,1,0:T(8,128)(2,1)} %collective-permute-done.3.xp_ref, bf16[512,1024]{1,0:T(8,128)(2,1)} %get-tuple-element.26.g_ref, ...), custom_call_target="tpu_custom_call" | custom-call | tf_op jit(solution)/shard_map/pallas_call | solution.py:303
  (17 shorter events, 0.0 us)
Async XLA Ops:
  0.6 19.6 %collective-permute-start.2 = (bf16[1024,1024]{1,0:T(8,128)(2,1)}, bf16[1024,1024]{1,0:T(8,128)(2,1)}, u32[]{:S(2)}, u32[]{:S(2)}) collective-permute-start(bf16[1024,1024]{1,0:T(8,128)(2,1)} %bitcast.35), channel_id=1, source_target_pairs={{0,64},{64,0},{1,65},{65,1},{2,66},{66,2},{3,67},{67,3},{4,68},{68... | collective-permute-start | bytes 6291464 | tf_op jit(solution)/shard_map/ppermute | solution.py:336
  5.0 39.0 %all-to-all-start = ((bf16[128,8,1024]{2,1,0:T(8,128)(2,1)}), bf16[128,8,1024]{2,1,0:T(8,128)(2,1)}, u32[]{:S(2)}, u32[]{:S(2)}) async-start(bf16[128,8,1024]{2,1,0:T(8,128)(2,1)} %bitcast.32), calls=%async_computation | async-start | bytes 4194304 | tf_op jit(solution)/shard_map/all_to_all | solution.py:339
  15.7 39.0 %collective-permute-start.1 = (bf16[2048,512]{1,0:T(8,128)(2,1)}, bf16[2048,512]{1,0:T(8,128)(2,1)}, u32[]{:S(2)}, u32[]{:S(2)}) collective-permute-start(bf16[2048,512]{1,0:T(8,128)(2,1)} %bitcast.4), channel_id=1, source_target_pairs={{0,64},{64,0},{1,65},{65,1},{2,66},{66,2},{3,67},{67,3},{4,68},{68... | collective-permute-start | bytes 6291464 | tf_op jit(solution)/shard_map/ppermute | solution.py:336
  16.9 40.3 %collective-permute-start = (bf16[2048,512]{1,0:T(8,128)(2,1)}, bf16[2048,512]{1,0:T(8,128)(2,1)}, u32[]{:S(2)}, u32[]{:S(2)}) collective-permute-start(bf16[2048,512]{1,0:T(8,128)(2,1)} %bitcast.3), channel_id=1, source_target_pairs={{0,64},{64,0},{1,65},{65,1},{2,66},{66,2},{3,67},{67,3},{4,68},{68... | collective-permute-start | bytes 6291464 | tf_op jit(solution)/shard_map/ppermute | solution.py:336
  44.0 34.7 %all-to-all-start.2 = ((bf16[128,8,1024]{2,1,0:T(8,128)(2,1)}), bf16[128,8,1024]{2,1,0:T(8,128)(2,1)S(1)}, u32[]{:S(2)}, u32[]{:S(2)}) async-start(bf16[128,8,1024]{2,1,0:T(8,128)(2,1)} %bitcast.31), calls=%async_computation.2 | async-start | bytes 4194304 | tf_op jit(solution)/shard_map/all_to_all | solution.py:339
  78.7 9.0 %copy-start = (bf16[128,8,1024]{2,1,0:T(8,128)(2,1)}, bf16[128,8,1024]{2,1,0:T(8,128)(2,1)S(1)}, u32[]{:S(2)}) copy-start(bf16[128,8,1024]{2,1,0:T(8,128)(2,1)S(1)} %all-to-all-done.2) | copy-start | bytes 6291460
  78.7 37.3 %all-to-all-start.1 = ((bf16[128,8,1024]{2,1,0:T(8,128)(2,1)}), bf16[128,8,1024]{2,1,0:T(8,128)(2,1)}, u32[]{:S(2)}, u32[]{:S(2)}) async-start(bf16[128,8,1024]{2,1,0:T(8,128)(2,1)} %bitcast.34), calls=%async_computation.1 | async-start | bytes 4194304 | tf_op jit(solution)/shard_map/all_to_all | solution.py:339
  87.7 42.2 %collective-permute-start.7 = (bf16[2,512,1024]{2,1,0:T(8,128)(2,1)S(1)}, bf16[2,512,1024]{2,1,0:T(8,128)(2,1)}, u32[]{:S(2)}, u32[]{:S(2)}) collective-permute-start(bf16[2,512,1024]{2,1,0:T(8,128)(2,1)S(1)} %bitcast.28), channel_id=1, source_target_pairs={{0,64},{64,0},{1,65},{65,1},{2,66},{66,2},{3,67},{67,3},{4,68},{68... | collective-permute-start | bytes 6291464 | tf_op jit(solution)/shard_map/ppermute | solution.py:336
  116.0 7.8 %copy-start.1 = (bf16[512,1024]{1,0:T(8,128)(2,1)S(1)}, bf16[512,1024]{1,0:T(8,128)(2,1)}, u32[]{:S(2)}) copy-start(bf16[512,1024]{1,0:T(8,128)(2,1)} %get-tuple-element.26.g_ref) | copy-start | bytes 3145732
  116.0 8.3 %copy-start.3 = (s32[160,2]{0,1:T(2,128)S(1)}, s32[160,2]{0,1:T(2,128)}, u32[]{:S(2)}) copy-start(s32[160,2]{0,1:T(2,128)} %param.8) | copy-start | bytes 3844
  116.0 9.1 %copy-start.4 = (f32[160,2]{0,1:T(2,128)S(1)}, f32[160,2]{0,1:T(2,128)}, u32[]{:S(2)}) copy-start(f32[160,2]{0,1:T(2,128)} %param.9) | copy-start | bytes 3844
  116.0 34.8 %all-to-all-start.3 = ((bf16[128,8,1024]{2,1,0:T(8,128)(2,1)}), bf16[128,8,1024]{2,1,0:T(8,128)(2,1)}, u32[]{:S(2)}, u32[]{:S(2)}) async-start(bf16[128,8,1024]{2,1,0:T(8,128)(2,1)} %bitcast.33), calls=%async_computation.3 | async-start | bytes 4194304 | tf_op jit(solution)/shard_map/all_to_all | solution.py:339
  122.5 31.2 %collective-permute-start.3 = (bf16[2,512,1024]{2,1,0:T(8,128)(2,1)}, bf16[2,512,1024]{2,1,0:T(8,128)(2,1)}, u32[]{:S(2)}, u32[]{:S(2)}) collective-permute-start(bf16[2,512,1024]{2,1,0:T(8,128)(2,1)} %bitcast.2.x_hbm.x_ref), channel_id=1, source_target_pairs={{0,64},{64,0},{1,65},{65,1},{2,66},{66,2},{3,67},{67,3},{4,68},{68... | collective-permute-start | bytes 6291464 | tf_op jit(solution)/shard_map/ppermute | solution.py:336
  123.7 6.2 %collective-permute-start.6 = (bf16[512,1024]{1,0:T(8,128)(2,1)}, bf16[512,1024]{1,0:T(8,128)(2,1)}, u32[]{:S(2)}, u32[]{:S(2)}) collective-permute-start(bf16[512,1024]{1,0:T(8,128)(2,1)} %get-tuple-element.30.h_ref), channel_id=1, source_target_pairs={{0,64},{64,0},{1,65},{65,1},{2,66},{66,2},{3,67},{67,3},{4,68},{68... | collective-permute-start | bytes 3145736 | tf_op jit(solution)/shard_map/ppermute | solution.py:336
  123.8 29.8 %collective-permute-start.4 = (bf16[512,1024]{1,0:T(8,128)(2,1)S(1)}, bf16[512,1024]{1,0:T(8,128)(2,1)}, u32[]{:S(2)}, u32[]{:S(2)}) collective-permute-start(bf16[512,1024]{1,0:T(8,128)(2,1)S(1)} %copy-done.1), channel_id=1, source_target_pairs={{0,64},{64,0},{1,65},{65,1},{2,66},{66,2},{3,67},{67,3},{4,68},{68... | collective-permute-start | bytes 3145736 | tf_op jit(solution)/shard_map/ppermute | solution.py:336
  124.2 29.4 %collective-permute-start.5 = (bf16[512,1024]{1,0:T(8,128)(2,1)}, bf16[512,1024]{1,0:T(8,128)(2,1)}, u32[]{:S(2)}, u32[]{:S(2)}) collective-permute-start(bf16[512,1024]{1,0:T(8,128)(2,1)} %get-tuple-element.27.u_ref), channel_id=1, source_target_pairs={{0,64},{64,0},{1,65},{65,1},{2,66},{66,2},{3,67},{67,3},{4,68},{68... | collective-permute-start | bytes 3145736 | tf_op jit(solution)/shard_map/ppermute | solution.py:336
  129.8 20.9 %copy-start.2 = (bf16[160,1024]{1,0:T(8,128)(2,1)S(1)}, bf16[160,1024]{1,0:T(8,128)(2,1)}, u32[]{:S(2)}) copy-start(bf16[160,1024]{1,0:T(8,128)(2,1)} %get-tuple-element.22) | copy-start | bytes 983044

commit v4 on v2

--- a/solution.py
+++ b/solution.py
@@ -15,6 +15,7 @@
 BLOCKS = 4
 HBM = pl.BlockSpec(memory_space=pl.ANY)
 VMEM = pl.BlockSpec(memory_space=pltpu.VMEM)
+GRANT = 64000 * 1024
 
 
 def dot(left, right, left_dims, right_dims):
@@ -48,11 +49,13 @@
     return slots
 
 
-def dispatch_kernel(weighted, experts, ids_ref, probs_ref, x_ref, out_ref):
+def dispatch_kernel(weighted, experts, ids_ref, probs_ref, x_ref, out_hbm, out_ref, sems):
     tok = x_ref.shape[0]
     chunk = out_ref.shape[0] // BLOCKS
     slots = slots_of([ids_ref[k : k + 1, :] for k in range(2)], 0, experts)
+    saves = []
     for n in range(BLOCKS):
+        here = pl.ds(n * chunk, chunk)
         spot = lax.broadcasted_iota(I32, (chunk, tok), 0) + n * chunk
         hits = [spot == slots[k] for k in range(2)]
         value = mm(one_hot(hits[0] | hits[1]), x_ref[...])
@@ -62,14 +65,21 @@
             )
             value = value * jnp.sum(probs, axis=1, keepdims=True)
         out_ref[n * chunk : (n + 1) * chunk, :] = value.astype(BF16)
+        saves.append(pltpu.make_async_copy(out_ref.at[here], out_hbm.at[here], sems.at[n]))
+        saves[n].start()
+    for save in saves:
+        save.wait()
 
 
 def dispatch(ids_t, probs_t, source, experts, weighted):
+    rows, width = 2 * experts * SUB, source.shape[1]
     return pl.pallas_call(
         functools.partial(dispatch_kernel, weighted, experts),
-        out_shape=jax.ShapeDtypeStruct((2 * experts * SUB, source.shape[1]), BF16),
+        out_shape=jax.ShapeDtypeStruct((rows, width), BF16),
         in_specs=[VMEM] * 3,
-        out_specs=VMEM,
+        out_specs=HBM,
+        scratch_shapes=[pltpu.VMEM((rows, width), BF16), pltpu.SemaphoreType.DMA((BLOCKS,))],
+        compiler_params=pltpu.CompilerParams(vmem_limit_bytes=GRANT) if weighted else None,
         name="send_grads" if weighted else "send_rows",
     )(ids_t, probs_t, source)
 
@@ -203,6 +213,7 @@
             pltpu.SemaphoreType.DMA,
             pltpu.SemaphoreType.DMA((2,)),
         ],
+        compiler_params=pltpu.CompilerParams(vmem_limit_bytes=GRANT),
         name="forward",
     )(rows_in, pair_weights, pair_weights, down_weights)
 

time: 169 us -> 170 us (level)
    unnamed x16 -> x14, local copies, waits for them, and re-layouts: 3.01 us -> 4.12 us
where the time goes in v4:
time: 170 us; the launch traced here: 169 us
  waiting for transfers between devices  55 us (32%)
  Pallas kernels  54.9 us (32%)
  starting transfers between devices  37.8 us (22%)
  other arithmetic  16.8 us (10%)
  local copies, waits for them, and re-layouts  4.12 us (2%)
    all_to_all x4, waiting for transfers between devices, exchange(): lax.all_to_all(value.reshape(2 * experts, SUB, width), ('dp', 'expert'),...  55 us
    all_to_all x4, starting transfers between devices, exchange(): lax.all_to_all(value.reshape(2 * experts, SUB, width), ('dp', 'expert'),...  31.8 us
    pallas_call x1, Pallas kernels, backward(): pl.pallas_call(backward_kernel, grid=(BLOCKS,), in_specs=[pl.BlockSpec((c...  15 us
    pallas_call x1, Pallas kernels, forward(): pl.pallas_call(forward_kernel, grid=(BLOCKS,), in_specs=[pl.BlockSpec(mem...  13.8 us
    pallas_call x2, Pallas kernels, share_call(): pl.pallas_call(kernel, out_shape=[shape] * outs, grid_spec=grid_spec)  13.4 us
    select_n x3, other arithmetic, in_order(): jnp.where(core == 0, mine, other)  8.81 us
    ppermute x8, starting transfers between devices, swap(): return lax.ppermute(value, 'dp', [(0, 1), (1, 0)])  5.93 us
    pallas_call x2, Pallas kernels, dispatch(): pl.pallas_call(functools.partial(dispatch_kernel, weighted, experts), out...  5.83 us
  transfers between devices with their start and end apart: 12, of which 4 were waited for; matrix products, arithmetic and copies ran while one was open for 11% of the time, Pallas kernels for 28%

profile of v4, /device:TPU:1, one launch (start us, length us, event | category | flops | bytes accessed | tf_op | source)
XLA Modules:
  0.0 169.4 jit_solution(1536977958322234675)
XLA Ops:
  0.6 1.5 collective-permute-start.2
  2.1 2.8 %send_rows.1 = bf16[1024,1024]{1,0:T(8,128)(2,1)} custom-call(s32[2,160]{1,0:T(2,128)} %bitcast.29, f32[2,160]{1,0:T(2,128)} %bitcast.31, bf16[160,1024]{1,0:T(8,128)(2,1)} %x_ref.2), custom_call_target="tpu_custom_call" | custom-call | tf_op jit(solution)/shard_map/send_rows/pallas_call | solution.py:76
  4.9 10.7 %all-to-all-start = ((bf16[128,8,1024]{2,1,0:T(8,128)(2,1)}), bf16[128,8,1024]{2,1,0:T(8,128)(2,1)}, u32[]{:S(2)}, u32[]{:S(2)}) async-start(bf16[128,8,1024]{2,1,0:T(8,128)(2,1)} %bitcast.24), calls=%async_computation | async-start | bytes 4194304 | tf_op jit(solution)/shard_map/all_to_all | solution.py:348
  15.6 1.2 collective-permute-start.1
  16.9 3.0 %send_grads.1 = bf16[1024,1024]{1,0:T(8,128)(2,1)} custom-call(s32[2,160]{1,0:T(2,128)} %bitcast.30, f32[2,160]{1,0:T(2,128)} %bitcast.32, bf16[160,1024]{1,0:T(8,128)(2,1)} %x_ref.3), custom_call_target="tpu_custom_call" | custom-call | tf_op jit(solution)/shard_map/send_grads/pallas_call | solution.py:76
  20.0 3.8 %broadcast_select_fusion.1 = (bf16[1024,1024]{1,0:T(8,128)(2,1)S(1)}, bf16[1024,1024]{1,0:T(8,128)(2,1)}) fusion(bf16[1024,1024]{1,0:T(8,128)(2,1)} %collective-permute-done.2, pred[]{:T(512)S(6)} %eq.2, bf16[1,1024,1024]{2,1,0:T(8,128)(2,1)} %param.13), kind=kLoop, calls=%fused_computation.3 | loop fusion | flops 2097152 | bytes 8388609 | tf_op jit(solution)/shard_map/jit(_where)/select_n | solution.py:357
  23.8 20.1 %all-to-all-done = bf16[128,8,1024]{2,1,0:T(8,128)(2,1)} async-done(((bf16[128,8,1024]{2,1,0:T(8,128)(2,1)}), bf16[128,8,1024]{2,1,0:T(8,128)(2,1)}, u32[]{:S(2)}, u32[]{:S(2)}) %all-to-all-start) | async-done | bytes 2097184 | tf_op jit(solution)/shard_map/all_to_all | solution.py:348
  43.9 6.5 %all-to-all-start.2 = ((bf16[128,8,1024]{2,1,0:T(8,128)(2,1)}), bf16[128,8,1024]{2,1,0:T(8,128)(2,1)}, u32[]{:S(2)}, u32[]{:S(2)}) async-start(bf16[128,8,1024]{2,1,0:T(8,128)(2,1)} %bitcast.9), calls=%async_computation.2 | async-start | bytes 4194304 | tf_op jit(solution)/shard_map/all_to_all | solution.py:348
  50.4 4.1 %pad_maximum_fusion.1.wd_hbm.wd_ref = bf16[1024,2048]{1,0:T(8,128)(2,1)} fusion(bf16[1024,1024]{1,0:T(8,128)(2,1)} %get-tuple-element.32, bf16[1024,1024]{1,0:T(8,128)(2,1)S(1)} %get-tuple-element.31), kind=kLoop, calls=%fused_computation.1 | loop fusion | flops 8388608 | bytes 8388608 | tf_op jit(solution)/shard_map/concatenate | solution.py:368
  54.5 2.5 %broadcast_select_fusion.3 = (bf16[2048,512]{1,0:T(8,128)(2,1)S(1)}, bf16[2048,512]{1,0:T(8,128)(2,1)S(1)}) fusion(bf16[2048,512]{1,0:T(8,128)(2,1)} %collective-permute-done.1, pred[]{:T(512)S(6)} %eq.2, bf16[1,2048,512]{2,1,0:T(8,128)(2,1)} %param.12), kind=kLoop, calls=%fused_computation.5 | loop fusion | flops 2097152 | bytes 8388609 | tf_op jit(solution)/shard_map/jit(_where)/select_n | solution.py:357
  57.0 2.5 %broadcast_select_fusion.5 = (bf16[2048,512]{1,0:T(8,128)(2,1)S(1)}, bf16[2048,512]{1,0:T(8,128)(2,1)S(1)}) fusion(bf16[2048,512]{1,0:T(8,128)(2,1)} %collective-permute-done, pred[]{:T(512)S(6)} %eq.2, bf16[1,2048,512]{2,1,0:T(8,128)(2,1)} %param.11), kind=kLoop, calls=%fused_computation.7 | loop fusion | flops 2097152 | bytes 8388609 | tf_op jit(solution)/shard_map/jit(_where)/select_n | solution.py:357
  59.5 3.9 %pad_maximum_fusion.wg_ref.wu_ref.wp_hbm = bf16[2048,2048]{1,0:T(8,128)(2,1)} fusion(bf16[2048,512]{1,0:T(8,128)(2,1)S(1)} %get-tuple-element.36, bf16[2048,512]{1,0:T(8,128)(2,1)S(1)} %get-tuple-element.35, bf16[2048,512]{1,0:T(8,128)(2,1)S(1)} %get-tuple-element.34, bf16[2048,512]{1,0:T(8,128)(2,1)S(1)} %get-tuple-element.33), kind=kLoop, calls=%fused_computation | loop fusion | flops 33554432 | bytes 16777216 | tf_op jit(solution)/shard_map/concatenate | solution.py:365
  63.4 13.8 %forward.1 = (f32[512,1024]{1,0:T(8,128)}, f32[512,1024]{1,0:T(8,128)}, bf16[512,1024]{1,0:T(8,128)(2,1)}, bf16[2,512,1024]{2,1,0:T(8,128)(2,1)}) custom-call(bf16[2,512,1024]{2,1,0:T(8,128)(2,1)} %bitcast.3.x_hbm.x_ref, bf16[2048,2048]{1,0:T(8,128)(2,1)} %pad_maximum_fusion.wg_ref.wu_ref.wp_hbm, bf16[2048,2048]{1,0:T(8,128)(2,1)} %pad_maximum_fusion.wg_ref.wu_ref.wp_hbm, ...), custom_call_target="tpu_custom_call" | custom-call | tf_op jit(solution)/shard_map/forward/pallas_call | solution.py:191
  77.2 1.5 all-to-all-done.2
  78.7 8.2 %all-to-all-start.1 = ((bf16[128,8,1024]{2,1,0:T(8,128)(2,1)}), bf16[128,8,1024]{2,1,0:T(8,128)(2,1)S(1)}, u32[]{:S(2)}, u32[]{:S(2)}) async-start(bf16[128,8,1024]{2,1,0:T(8,128)(2,1)} %bitcast.26), calls=%async_computation.1 | async-start | bytes 4194304 | tf_op jit(solution)/shard_map/all_to_all | solution.py:348
  86.9 1.1 collective-permute-start.7
  88.1 0.3 collective-permute-start.3
  88.4 15.0 %backward.1 = (bf16[512,1024]{1,0:T(8,128)(2,1)}, bf16[512,1024]{1,0:T(8,128)(2,1)}, bf16[2,512,1024]{2,1,0:T(8,128)(2,1)}) custom-call(bf16[2,512,1024]{2,1,0:T(8,128)(2,1)} %bitcast.10.g_ref, f32[512,1024]{1,0:T(8,128)} %get-tuple-element.23.gp_ref, f32[512,1024]{1,0:T(8,128)} %get-tuple-element.24.up_ref, ...), custom_call_target="tpu_custom_call" | custom-call | tf_op jit(solution)/shard_map/backward/pallas_call | solution.py:263
  103.3 12.3 %all-to-all-done.1 = bf16[128,8,1024]{2,1,0:T(8,128)(2,1)S(1)} async-done(((bf16[128,8,1024]{2,1,0:T(8,128)(2,1)}), bf16[128,8,1024]{2,1,0:T(8,128)(2,1)S(1)}, u32[]{:S(2)}, u32[]{:S(2)}) %all-to-all-start.1) | async-done | bytes 2097184 | tf_op jit(solution)/shard_map/all_to_all | solution.py:348
  115.6 1.3 copy-done
  116.9 6.5 %all-to-all-start.3 = ((bf16[128,8,1024]{2,1,0:T(8,128)(2,1)}), bf16[128,8,1024]{2,1,0:T(8,128)(2,1)}, u32[]{:S(2)}, u32[]{:S(2)}) async-start(bf16[128,8,1024]{2,1,0:T(8,128)(2,1)} %bitcast.25), calls=%async_computation.3 | async-start | bytes 4194304 | tf_op jit(solution)/shard_map/all_to_all | solution.py:348
  123.4 1.2 collective-permute-start.6
  124.7 0.4 collective-permute-start.5
  125.1 0.8 copy.12.ids_ref
  125.9 0.8 copy.13.probs_ref
  126.7 4.0 %mix.1 = (bf16[160,1024]{1,0:T(8,128)(2,1)}, bf16[160,1024]{1,0:T(8,128)(2,1)}) custom-call(s32[160,2]{1,0:T(8,128)} %copy.12.ids_ref, f32[160,2]{1,0:T(8,128)} %copy.13.probs_ref, bf16[1024,1024]{1,0:T(8,128)(2,1)} %bitcast.23), custom_call_target="tpu_custom_call" | custom-call | tf_op jit(solution)/shard_map/mix/pallas_call | solution.py:111
  130.7 21.0 %all-to-all-done.3 = bf16[128,8,1024]{2,1,0:T(8,128)(2,1)} async-done(((bf16[128,8,1024]{2,1,0:T(8,128)(2,1)}), bf16[128,8,1024]{2,1,0:T(8,128)(2,1)}, u32[]{:S(2)}, u32[]{:S(2)}) %all-to-all-start.3) | async-done | bytes 2097184 | tf_op jit(solution)/shard_map/all_to_all | solution.py:348
  151.7 3.0 %add_routes.1 = bf16[160,1024]{1,0:T(8,128)(2,1)} custom-call(bf16[160,1024]{1,0:T(8,128)(2,1)} %get-tuple-element.22.select_ref, bf16[1024,1024]{1,0:T(8,128)(2,1)} %bitcast.12.back_ref), custom_call_target="tpu_custom_call" | custom-call | tf_op jit(solution)/shard_map/add_routes/pallas_call | solution.py:128
  154.7 5.4 %shard_map.111 = bf16[1024,1024]{1,0:T(8,128)(2,1)} custom-call(s32[1]{0:T(128)} %bitcast.13.core_ref, bf16[512,1024]{1,0:T(8,128)(2,1)} %get-tuple-element.30.h_ref, bf16[512,1024]{1,0:T(8,128)(2,1)} %collective-permute-done.6.hp_ref, bf16[2,512,1024]{2,1,0:T(8,128)(2,1)} %bitcast.10.g_ref, bf16[2,512,1024]{2,1,0:T(8,128)(2,1)} %collective-permute-done.7.gp_ref), custom_call_target="tpu_custom_call" | custom-call | tf_op jit(solution)/shard_map/pallas_call | solution.py:312
  160.1 1.0 copy-done.2
  161.1 0.3 copy-done.3
  161.4 7.9 %shard_map.110 = (bf16[2048,512]{1,0:T(8,128)(2,1)}, bf16[2048,512]{1,0:T(8,128)(2,1)}) custom-call(s32[1]{0:T(128)} %bitcast.13.core_ref, bf16[2,512,1024]{2,1,0:T(8,128)(2,1)} %bitcast.3.x_hbm.x_ref, bf16[2,512,1024]{2,1,0:T(8,128)(2,1)} %collective-permute-done.3.xp_ref, bf16[512,1024]{1,0:T(8,128)(2,1)} %get-tuple-element.26.g_ref, ...), custom_call_target="tpu_custom_call" | custom-call | tf_op jit(solution)/shard_map/pallas_call | solution.py:312
  (19 shorter events, 0.2 us)
Async XLA Ops:
  0.6 19.3 %collective-permute-start.2 = (bf16[1024,1024]{1,0:T(8,128)(2,1)}, bf16[1024,1024]{1,0:T(8,128)(2,1)}, u32[]{:S(2)}, u32[]{:S(2)}) collective-permute-start(bf16[1024,1024]{1,0:T(8,128)(2,1)} %bitcast.27), channel_id=1, source_target_pairs={{0,64},{64,0},{1,65},{65,1},{2,66},{66,2},{3,67},{67,3},{4,68},{68... | collective-permute-start | bytes 6291464 | tf_op jit(solution)/shard_map/ppermute | solution.py:345
  4.9 39.0 %all-to-all-start = ((bf16[128,8,1024]{2,1,0:T(8,128)(2,1)}), bf16[128,8,1024]{2,1,0:T(8,128)(2,1)}, u32[]{:S(2)}, u32[]{:S(2)}) async-start(bf16[128,8,1024]{2,1,0:T(8,128)(2,1)} %bitcast.24), calls=%async_computation | async-start | bytes 4194304 | tf_op jit(solution)/shard_map/all_to_all | solution.py:348
  15.6 38.9 %collective-permute-start.1 = (bf16[2048,512]{1,0:T(8,128)(2,1)}, bf16[2048,512]{1,0:T(8,128)(2,1)}, u32[]{:S(2)}, u32[]{:S(2)}) collective-permute-start(bf16[2048,512]{1,0:T(8,128)(2,1)} %bitcast.5), channel_id=1, source_target_pairs={{0,64},{64,0},{1,65},{65,1},{2,66},{66,2},{3,67},{67,3},{4,68},{68... | collective-permute-start | bytes 6291464 | tf_op jit(solution)/shard_map/ppermute | solution.py:345
  16.8 40.2 %collective-permute-start = (bf16[2048,512]{1,0:T(8,128)(2,1)}, bf16[2048,512]{1,0:T(8,128)(2,1)}, u32[]{:S(2)}, u32[]{:S(2)}) collective-permute-start(bf16[2048,512]{1,0:T(8,128)(2,1)} %bitcast.4), channel_id=1, source_target_pairs={{0,64},{64,0},{1,65},{65,1},{2,66},{66,2},{3,67},{67,3},{4,68},{68... | collective-permute-start | bytes 6291464 | tf_op jit(solution)/shard_map/ppermute | solution.py:345
  43.9 34.8 %all-to-all-start.2 = ((bf16[128,8,1024]{2,1,0:T(8,128)(2,1)}), bf16[128,8,1024]{2,1,0:T(8,128)(2,1)}, u32[]{:S(2)}, u32[]{:S(2)}) async-start(bf16[128,8,1024]{2,1,0:T(8,128)(2,1)} %bitcast.9), calls=%async_computation.2 | async-start | bytes 4194304 | tf_op jit(solution)/shard_map/all_to_all | solution.py:348
  78.7 36.9 %all-to-all-start.1 = ((bf16[128,8,1024]{2,1,0:T(8,128)(2,1)}), bf16[128,8,1024]{2,1,0:T(8,128)(2,1)S(1)}, u32[]{:S(2)}, u32[]{:S(2)}) async-start(bf16[128,8,1024]{2,1,0:T(8,128)(2,1)} %bitcast.26), calls=%async_computation.1 | async-start | bytes 4194304 | tf_op jit(solution)/shard_map/all_to_all | solution.py:348
  86.9 67.7 %collective-permute-start.7 = (bf16[2,512,1024]{2,1,0:T(8,128)(2,1)}, bf16[2,512,1024]{2,1,0:T(8,128)(2,1)}, u32[]{:S(2)}, u32[]{:S(2)}) collective-permute-start(bf16[2,512,1024]{2,1,0:T(8,128)(2,1)} %bitcast.10.g_ref), channel_id=1, source_target_pairs={{0,64},{64,0},{1,65},{65,1},{2,66},{66,2},{3,67},{67,3},{4,68},{68... | collective-permute-start | bytes 6291464 | tf_op jit(solution)/shard_map/ppermute | solution.py:345
  88.1 72.1 %collective-permute-start.3 = (bf16[2,512,1024]{2,1,0:T(8,128)(2,1)}, bf16[2,512,1024]{2,1,0:T(8,128)(2,1)}, u32[]{:S(2)}, u32[]{:S(2)}) collective-permute-start(bf16[2,512,1024]{2,1,0:T(8,128)(2,1)} %bitcast.3.x_hbm.x_ref), channel_id=1, source_target_pairs={{0,64},{64,0},{1,65},{65,1},{2,66},{66,2},{3,67},{67,3},{4,68},{68... | collective-permute-start | bytes 6291464 | tf_op jit(solution)/shard_map/ppermute | solution.py:345
  115.6 1.3 copy-start
  115.6 7.8 %copy-start.1 = (bf16[512,1024]{1,0:T(8,128)(2,1)S(1)}, bf16[512,1024]{1,0:T(8,128)(2,1)}, u32[]{:S(2)}) copy-start(bf16[512,1024]{1,0:T(8,128)(2,1)} %get-tuple-element.30.h_ref) | copy-start | bytes 3145732
  115.6 9.5 %copy-start.4 = (s32[160,2]{0,1:T(2,128)S(1)}, s32[160,2]{0,1:T(2,128)}, u32[]{:S(2)}) copy-start(s32[160,2]{0,1:T(2,128)} %param.8) | copy-start | bytes 3844
  115.6 10.3 %copy-start.5 = (f32[160,2]{0,1:T(2,128)S(1)}, f32[160,2]{0,1:T(2,128)}, u32[]{:S(2)}) copy-start(f32[160,2]{0,1:T(2,128)} %param.9) | copy-start | bytes 3844
  116.9 34.8 %all-to-all-start.3 = ((bf16[128,8,1024]{2,1,0:T(8,128)(2,1)}), bf16[128,8,1024]{2,1,0:T(8,128)(2,1)}, u32[]{:S(2)}, u32[]{:S(2)}) async-start(bf16[128,8,1024]{2,1,0:T(8,128)(2,1)} %bitcast.25), calls=%async_computation.3 | async-start | bytes 4194304 | tf_op jit(solution)/shard_map/all_to_all | solution.py:348
  123.4 31.3 %collective-permute-start.6 = (bf16[512,1024]{1,0:T(8,128)(2,1)S(1)}, bf16[512,1024]{1,0:T(8,128)(2,1)}, u32[]{:S(2)}, u32[]{:S(2)}) collective-permute-start(bf16[512,1024]{1,0:T(8,128)(2,1)S(1)} %copy-done.1), channel_id=1, source_target_pairs={{0,64},{64,0},{1,65},{65,1},{2,66},{66,2},{3,67},{67,3},{4,68},{68... | collective-permute-start | bytes 3145736 | tf_op jit(solution)/shard_map/ppermute | solution.py:345
  124.6 35.5 %collective-permute-start.4 = (bf16[512,1024]{1,0:T(8,128)(2,1)}, bf16[512,1024]{1,0:T(8,128)(2,1)S(1)}, u32[]{:S(2)}, u32[]{:S(2)}) collective-permute-start(bf16[512,1024]{1,0:T(8,128)(2,1)} %get-tuple-element.26.g_ref), channel_id=1, source_target_pairs={{0,64},{64,0},{1,65},{65,1},{2,66},{66,2},{3,67},{67,3},{4,68},{68... | collective-permute-start | bytes 3145736 | tf_op jit(solution)/shard_map/ppermute | solution.py:345
  124.7 35.4 %collective-permute-start.5 = (bf16[512,1024]{1,0:T(8,128)(2,1)}, bf16[512,1024]{1,0:T(8,128)(2,1)S(1)}, u32[]{:S(2)}, u32[]{:S(2)}) collective-permute-start(bf16[512,1024]{1,0:T(8,128)(2,1)} %get-tuple-element.27.u_ref), channel_id=1, source_target_pairs={{0,64},{64,0},{1,65},{65,1},{2,66},{66,2},{3,67},{67,3},{4,68},{68... | collective-permute-start | bytes 3145736 | tf_op jit(solution)/shard_map/ppermute | solution.py:345
  160.1 1.0 copy-start.2
  160.1 1.3 copy-start.3
